TPU v7x, 512 devices: a whole 4x4x16 slice. The times are simulated.
512 devices in a mesh: req: 128 (over x, z, core), tp: 4 (over y).
Axes of the slice: x: 4, y: 4, z: 16, core: 2. Of those that a mesh axis runs over, the one named last changes fastest.
Arguments:
- layer_input: bfloat16 [16384, 2048], P('req', 'tp'), may hold values from -6 to 6
- q_in: bfloat16 [16384, 1024], P('req', 'tp'), may hold values from -6 to 6
- k_in: bfloat16 [16384, 1024], P('req', 'tp'), may hold values from -6 to 6
- v_in: bfloat16 [16384, 2048], P('req', 'tp'), may hold values from -6 to 6
- z_in: bfloat16 [16384, 2048], P('req', 'tp'), may hold values from -6 to 6
- conv_q: bfloat16 [4, 1024], P(None, 'tp'), may hold values from -3 to 3
- conv_k: bfloat16 [4, 1024], P(None, 'tp'), may hold values from -3 to 3
- conv_v: bfloat16 [4, 2048], P(None, 'tp'), may hold values from -3 to 3
- gate_weight: bfloat16 [2048, 16], P('tp'), may hold values from -0.125 to 0.125
- decay_rate: float32 [8], P('tp'), may hold values from 0.0001 to 0.05
- dt_bias: float32 [8], P('tp'), may hold values from -1 to 1
- norm_gain: bfloat16 [256], replicated, may hold values from 0.099609375 to 1.8984375
- segment_ids: int32 [16384], P('req'), may hold values from 0 to 63, never falling along the last dimension, each value on 1 to 1024 neighbouring positions
Outputs:
- mixed: bfloat16 [16384, 2048], P('req', 'tp')
Inputs may be any that keep to these rules, and one draw needn't show every extreme that they name: segment_ids never falls along the tokens; every prompt 0 to 63 has 1 to 1024 tokens, and one has exactly 1024.
All inputs are finite; a program needn't handle non-finite values.
Results may differ from a plain program's by a relative error of at most 0.0055.
Values may be sent and summed in bfloat16 or wider, within the bound.
A program may use at most 128 MiB of HBM per device.

v0:
```python
import jax
import jax.numpy as jnp
from jax import lax
from jax.sharding import PartitionSpec as P

HEADS = 8
DK = 128
DV = 256
CONV = 4
BLOCK = 64


highest = lax.Precision.HIGHEST


def passed_along(value, axis, by):
    devices = lax.axis_size(axis)
    pairs = [(i, i + by) for i in range(devices) if 0 <= i + by < devices]
    return lax.ppermute(value, axis, pairs)


def product(pattern, first_op, second_op):
    return jnp.einsum(pattern, first_op, second_op, precision=highest)


def short_conv(extended, seg_ext, weight, row_count):
    own_seg = seg_ext[CONV - 1 :]
    summed = jnp.zeros((row_count, extended.shape[1]), jnp.float32)
    for offset in range(CONV):
        same_req = (seg_ext[offset : offset + row_count] == own_seg)[:, None]
        summed = summed + jnp.where(same_req, extended[offset : offset + row_count], 0.0) * weight[
            offset
        ].astype(jnp.float32)
    return jax.nn.silu(summed)


def unit_keys(key_raw, heads):
    shaped = key_raw.reshape(key_raw.shape[0], heads, DK)
    return shaped * lax.rsqrt(jnp.sum(shaped * shaped, axis=2, keepdims=True) + 1e-06)


def block_terms(queries, keyset, values, log_alpha, beta_gate, seg_block, seg_before):
    length = seg_block.shape[0]
    width = values.shape[2]
    cumulative = jnp.cumsum(log_alpha, axis=0)
    positions = jnp.arange(length)
    same_req = seg_block[:, None] == seg_block[None, :]
    causal = (positions[:, None] >= positions[None, :]) & same_req
    strict = (positions[:, None] > positions[None, :]) & same_req
    gap_log = jnp.transpose(cumulative[:, None, :] - cumulative[None, :, :], (2, 0, 1))
    decays = jnp.where(causal[None], jnp.exp(jnp.where(causal[None], gap_log, 0.0)), 0.0)
    linked = (seg_block == seg_before).astype(jnp.float32)
    tail_mask = (seg_block == seg_block[length - 1]).astype(jnp.float32)
    key_dots = product("ihd,jhd->hij", keyset, keyset)
    coupling = (
        jnp.transpose(beta_gate)[:, :, None] * key_dots * jnp.where(strict[None], decays, 0.0)
    )
    system = jnp.eye(length, dtype=jnp.float32)[None] + coupling
    start_scale = jnp.exp(cumulative) * linked[:, None]
    right_side = jnp.concatenate(
        [beta_gate[:, :, None] * values, (beta_gate * start_scale)[:, :, None] * keyset], axis=2
    )
    solved = lax.linalg.triangular_solve(
        system, jnp.transpose(right_side, (1, 0, 2)), left_side=True, lower=True
    )
    fresh_part = solved[:, :, :width]
    carried = solved[:, :, width:]
    scores = product("ihd,jhd->hij", queries, keyset) * decays
    reach_back = jnp.transpose(queries * start_scale[:, :, None], (1, 0, 2)) - product(
        "hij,hjd->hid", scores, carried
    )
    local_out = product("hij,hjd->hid", scores, fresh_part)
    fade_out = jnp.exp(cumulative[length - 1][None, :] - cumulative) * tail_mask[:, None]
    pushed = jnp.transpose(fade_out[:, :, None] * keyset, (1, 0, 2))
    keep_scale = linked[length - 1] * jnp.exp(cumulative[length - 1])
    carry_map = keep_scale[:, None, None] * jnp.eye(keyset.shape[2], dtype=jnp.float32)[
        None
    ] - product("hcd,hce->hde", pushed, carried)
    injected = product("hcd,hce->hde", pushed, fresh_part)
    return (local_out, reach_back, carry_map, injected)


def finish(outputs, z_part, norm_gain):
    scale = lax.rsqrt(jnp.mean(outputs * outputs, axis=2, keepdims=True) + 1e-06)
    gating = jax.nn.silu(z_part.astype(jnp.float32).reshape(outputs.shape))
    result = outputs * scale * norm_gain.astype(jnp.float32)[None, None, :] * gating
    return result.astype(jnp.bfloat16).reshape(outputs.shape[0], -1)


def local(
    layer_input,
    q_in,
    k_in,
    v_in,
    z_in,
    conv_q,
    conv_k,
    conv_v,
    gate_weight,
    decay_rate,
    dt_bias,
    norm_gain,
    segment_ids,
):
    row_count = q_in.shape[0]
    local_heads = q_in.shape[1] // DK
    edge_rows = CONV - 1
    seg_marks = (segment_ids[row_count - edge_rows :] + 1).astype(jnp.bfloat16)
    prior_q, prior_k, prior_v, prior_marks = passed_along(
        (
            q_in[row_count - edge_rows :],
            k_in[row_count - edge_rows :],
            v_in[row_count - edge_rows :],
            seg_marks,
        ),
        "req",
        1,
    )
    prior_seg = prior_marks.astype(jnp.int32) - 1
    seg_ext = jnp.concatenate([prior_seg, segment_ids])
    queries = short_conv(
        jnp.concatenate([prior_q, q_in]).astype(jnp.float32), seg_ext, conv_q, row_count
    )
    keyset = unit_keys(
        short_conv(
            jnp.concatenate([prior_k, k_in]).astype(jnp.float32), seg_ext, conv_k, row_count
        ),
        local_heads,
    )
    values = short_conv(
        jnp.concatenate([prior_v, v_in]).astype(jnp.float32), seg_ext, conv_v, row_count
    )
    partial_value = jnp.dot(layer_input, gate_weight, preferred_element_type=jnp.float32)
    gate_total = lax.psum(partial_value, "tp")
    head_start = lax.axis_index("tp") * local_heads
    decay_in = lax.dynamic_slice_in_dim(gate_total, head_start, local_heads, 1)
    beta_in = lax.dynamic_slice_in_dim(gate_total, HEADS + head_start, local_heads, 1)
    log_alpha = -decay_rate[None, :] * jax.nn.softplus(decay_in + dt_bias[None, :])
    beta_gate = jax.nn.sigmoid(beta_in)
    block_count = row_count // BLOCK
    previous = jnp.concatenate([prior_seg[edge_rows - 1 :], segment_ids[:-1]])
    seg_starts = previous.reshape(block_count, BLOCK)[:, 0]

    def blocks(array):
        return array.reshape((block_count, BLOCK) + array.shape[1:])

    def sweep_block(running, block_data):
        carry_acc, inject_acc = running
        q_part, k_part, v_part, alpha_part, beta_part, seg_part, seg_before = block_data
        local_out, reach_back, carry_map, injected = block_terms(
            q_part, k_part, v_part, alpha_part, beta_part, seg_part, seg_before
        )
        own_out = local_out + product("hcd,hde->hce", reach_back, inject_acc)
        lead_map = product("hcd,hde->hce", reach_back, carry_acc)
        next_running = (
            product("hde,hef->hdf", carry_map, carry_acc),
            product("hde,hef->hdf", carry_map, inject_acc) + injected,
        )
        return (next_running, (own_out, lead_map))

    identity = jnp.broadcast_to(jnp.eye(DK, dtype=jnp.float32), (local_heads, DK, DK))
    empty = jnp.zeros((local_heads, DK, DV), jnp.float32)
    block_data = (
        blocks(queries.reshape(row_count, local_heads, DK)),
        blocks(keyset),
        blocks(values.reshape(row_count, local_heads, DV)),
        blocks(log_alpha),
        blocks(beta_gate),
        blocks(segment_ids),
        seg_starts,
    )
    totals, outputs = lax.scan(sweep_block, (identity, empty), block_data)
    carry_total, inject_total = totals
    own_out, lead_map = outputs
    span = min(8, lax.axis_size("req") // 2)
    incoming = empty
    for hop_index in range(span):
        incoming = passed_along(
            product("hde,hef->hdf", carry_total, incoming) + inject_total, "req", 1
        )
    head_out = own_out + product("nhcd,hde->nhce", lead_map, incoming)
    head_out = jnp.transpose(head_out, (0, 2, 1, 3)).reshape(row_count, local_heads, DV)
    return finish(head_out, z_in, norm_gain)


def solution(mesh):
    placed = (
        P("req", "tp"),
        P("req", "tp"),
        P("req", "tp"),
        P("req", "tp"),
        P("req", "tp"),
        P(None, "tp"),
        P(None, "tp"),
        P(None, "tp"),
        P("tp", None),
        P("tp"),
        P("tp"),
        P(),
        P("req"),
    )
    return jax.shard_map(
        local, mesh=mesh, in_specs=placed, out_specs=P("req", "tp"), check_vma=False
    )
```

profile of v0, /device:TPU:6, one launch (start us, length us, event | category | flops | bytes accessed | tf_op | source)
XLA Modules:
  0.0 152.9 jit_solution(2197556349249969741)
XLA Ops:
  0.0 0.8 add_convert_fusion
  0.8 1.9 %collective-permute-start = (bf16[3]{0:T(256)(128)(2,1)S(1)}, bf16[3]{0:T(256)(128)(2,1)S(1)}, u32[]{:S(2)}, u32[]{:S(2)}) collective-permute-start(bf16[3]{0:T(256)(128)(2,1)S(1)} %add_convert_fusion), channel_id=1, source_target_pairs={{0,4},{4,8},{8,12},{12,16},{16,20},{20,24},{24,28},{28,32},{32,36}... | collective-permute-start | bytes 26 | tf_op jit(solution)/shard_map/ppermute | solution.py:19
  2.7 0.7 slice.134
  3.4 3.9 %collective-permute-start.1 = (bf16[3,256]{1,0:T(4,128)(2,1)S(1)}, bf16[3,256]{1,0:T(4,128)(2,1)S(1)}, u32[]{:S(2)}, u32[]{:S(2)}) collective-permute-start(bf16[3,256]{1,0:T(4,128)(2,1)S(1)} %slice.134), channel_id=1, source_target_pairs={{0,4},{4,8},{8,12},{12,16},{16,20},{20,24},{24,28},{28,32},{32,36}... | collective-permute-start | bytes 4616 | tf_op jit(solution)/shard_map/ppermute | solution.py:19
  7.3 0.7 slice.154
  8.0 1.9 %collective-permute-start.3 = (bf16[3,256]{1,0:T(4,128)(2,1)S(1)}, bf16[3,256]{1,0:T(4,128)(2,1)S(1)}, u32[]{:S(2)}, u32[]{:S(2)}) collective-permute-start(bf16[3,256]{1,0:T(4,128)(2,1)S(1)} %slice.154), channel_id=1, source_target_pairs={{0,4},{4,8},{8,12},{12,16},{16,20},{20,24},{24,28},{28,32},{32,36}... | collective-permute-start | bytes 4616 | tf_op jit(solution)/shard_map/ppermute | solution.py:19
  9.9 0.7 slice.145
  10.6 3.9 %collective-permute-start.2 = (bf16[3,512]{1,0:T(4,128)(2,1)S(1)}, bf16[3,512]{1,0:T(4,128)(2,1)S(1)}, u32[]{:S(2)}, u32[]{:S(2)}) collective-permute-start(bf16[3,512]{1,0:T(4,128)(2,1)S(1)} %slice.145), channel_id=1, source_target_pairs={{0,4},{4,8},{8,12},{12,16},{16,20},{20,24},{24,28},{28,32},{32,36}... | collective-permute-start | bytes 9224 | tf_op jit(solution)/shard_map/ppermute | solution.py:19
  14.6 0.6 copy-done.9
  15.3 0.6 copy-done.8
  16.2 11.0 %psum.7 = f32[128,16]{0,1:T(8,128)S(1)} all-reduce(f32[128,16]{0,1:T(8,128)S(1)} %fusion.69), channel_id=1, replica_groups=mesh['req'=128,'tp'=4] {'tp'}, use_global_device_ids=true, to_apply=%region_1.2 | all-reduce | flops 2048 | bytes 16384 | tf_op jit(solution)/shard_map/psum | solution.py:134
  27.6 0.6 slice.130
  28.3 0.7 pad_add_fusion.1
  29.2 0.8 copy-done.4
  31.0 0.8 copy-done.1
  32.3 36.5 %while.17 = (s32[]{:T(128)}, f32[2,128,128]{2,1,0:T(8,128)S(1)}, f32[2,128,256]{2,1,0:T(8,128)S(1)}, f32[2,2,64,256]{3,2,0,1:T(8,128)S(1)}, f32[2,2,64,128]{3,2,...) while((s32[]{:T(128)}, f32[2,128,128]{2,1,0:T(8,128)S(1)}, ...), condition=%wide.region_4.5_spmd.clone, body=%wide.region_2.4_spmd.clone.sunk | while | flops 403280512 | bytes 5553924 | solution.py:172
  32.3 0.7 dynamic_slice.57
  33.0 0.6 compare_convert_fusion.4
  33.6 0.6 slice.320
  34.3 0.6 compare_convert_fusion.5
  35.9 9.8 %custom-call.8 = f32[2,1,64,64]{2,3,1,0:T(8,128)S(1)} custom-call(f32[2,1,64,64]{3,2,1,0:T(8,128)S(1)} %fusion.147), custom_call_target="InvertDiagBlocksLowerTriangular" | custom-call | tf_op jit(solution)/shard_map/while/body/eval_jaxpr/triangular_solve | solution.py:63
  47.4 0.7 slice.319
  48.0 0.6 exponential_multiply_fusion.5
  50.6 0.7 dynamic_slice.57
  51.3 0.6 compare_convert_fusion.4
  51.9 0.6 slice.320
  52.5 0.6 compare_convert_fusion.5
  54.2 9.8 %custom-call.8 = f32[2,1,64,64]{2,3,1,0:T(8,128)S(1)} custom-call(f32[2,1,64,64]{3,2,1,0:T(8,128)S(1)} %fusion.147), custom_call_target="InvertDiagBlocksLowerTriangular" | custom-call | tf_op jit(solution)/shard_map/while/body/eval_jaxpr/triangular_solve | solution.py:63
  65.7 0.7 slice.319
  66.3 0.6 exponential_multiply_fusion.5
  69.1 1.9 %collective-permute-start.4 = (f32[2,128,256]{2,1,0:T(8,128)S(1)}, f32[2,128,256]{2,1,0:T(8,128)S(1)}, u32[]{:S(2)}, u32[]{:S(2)}) collective-permute-start(f32[2,128,256]{2,1,0:T(8,128)S(1)} %convolution_add_fusion.9), channel_id=1, source_target_pairs={{0,4},{4,8},{8,12},{12,16},{16,20},{20,24},{24,28},{28,32},{32,36}... | collective-permute-start | bytes 786440 | tf_op jit(solution)/shard_map/ppermute | solution.py:19
  71.1 7.9 %collective-permute-done.4 = f32[2,128,256]{2,1,0:T(8,128)S(1)} collective-permute-done((f32[2,128,256]{2,1,0:T(8,128)S(1)}, f32[2,128,256]{2,1,0:T(8,128)S(1)}, u32[]{:S(2)}, u32[]{:S(2)}) %collective-permute-start.4) | collective-permute-done | bytes 262176 | tf_op jit(solution)/shard_map/ppermute | solution.py:19
  79.3 1.9 %collective-permute-start.5 = (f32[2,128,256]{2,1,0:T(8,128)S(1)}, f32[2,128,256]{2,1,0:T(8,128)S(1)}, u32[]{:S(2)}, u32[]{:S(2)}) collective-permute-start(f32[2,128,256]{2,1,0:T(8,128)S(1)} %convolution_add_fusion.8), channel_id=1, source_target_pairs={{0,4},{4,8},{8,12},{12,16},{16,20},{20,24},{24,28},{28,32},{32,36}... | collective-permute-start | bytes 786440 | tf_op jit(solution)/shard_map/ppermute | solution.py:19
  81.2 7.9 %collective-permute-done.5 = f32[2,128,256]{2,1,0:T(8,128)S(1)} collective-permute-done((f32[2,128,256]{2,1,0:T(8,128)S(1)}, f32[2,128,256]{2,1,0:T(8,128)S(1)}, u32[]{:S(2)}, u32[]{:S(2)}) %collective-permute-start.5) | collective-permute-done | bytes 262176 | tf_op jit(solution)/shard_map/ppermute | solution.py:19
  89.5 1.9 %collective-permute-start.6 = (f32[2,128,256]{2,1,0:T(8,128)S(1)}, f32[2,128,256]{2,1,0:T(8,128)S(1)}, u32[]{:S(2)}, u32[]{:S(2)}) collective-permute-start(f32[2,128,256]{2,1,0:T(8,128)S(1)} %convolution_add_fusion.7), channel_id=1, source_target_pairs={{0,4},{4,8},{8,12},{12,16},{16,20},{20,24},{24,28},{28,32},{32,36}... | collective-permute-start | bytes 786440 | tf_op jit(solution)/shard_map/ppermute | solution.py:19
  91.4 7.9 %collective-permute-done.6 = f32[2,128,256]{2,1,0:T(8,128)S(1)} collective-permute-done((f32[2,128,256]{2,1,0:T(8,128)S(1)}, f32[2,128,256]{2,1,0:T(8,128)S(1)}, u32[]{:S(2)}, u32[]{:S(2)}) %collective-permute-start.6) | collective-permute-done | bytes 262176 | tf_op jit(solution)/shard_map/ppermute | solution.py:19
  99.6 1.9 %collective-permute-start.7 = (f32[2,128,256]{2,1,0:T(8,128)S(1)}, f32[2,128,256]{2,1,0:T(8,128)S(1)}, u32[]{:S(2)}, u32[]{:S(2)}) collective-permute-start(f32[2,128,256]{2,1,0:T(8,128)S(1)} %convolution_add_fusion.6), channel_id=1, source_target_pairs={{0,4},{4,8},{8,12},{12,16},{16,20},{20,24},{24,28},{28,32},{32,36}... | collective-permute-start | bytes 786440 | tf_op jit(solution)/shard_map/ppermute | solution.py:19
  101.6 7.9 %collective-permute-done.7 = f32[2,128,256]{2,1,0:T(8,128)S(1)} collective-permute-done((f32[2,128,256]{2,1,0:T(8,128)S(1)}, f32[2,128,256]{2,1,0:T(8,128)S(1)}, u32[]{:S(2)}, u32[]{:S(2)}) %collective-permute-start.7) | collective-permute-done | bytes 262176 | tf_op jit(solution)/shard_map/ppermute | solution.py:19
  109.8 1.9 %collective-permute-start.8 = (f32[2,128,256]{2,1,0:T(8,128)S(1)}, f32[2,128,256]{2,1,0:T(8,128)S(1)}, u32[]{:S(2)}, u32[]{:S(2)}) collective-permute-start(f32[2,128,256]{2,1,0:T(8,128)S(1)} %convolution_add_fusion.5), channel_id=1, source_target_pairs={{0,4},{4,8},{8,12},{12,16},{16,20},{20,24},{24,28},{28,32},{32,36}... | collective-permute-start | bytes 786440 | tf_op jit(solution)/shard_map/ppermute | solution.py:19
  111.8 7.9 %collective-permute-done.8 = f32[2,128,256]{2,1,0:T(8,128)S(1)} collective-permute-done((f32[2,128,256]{2,1,0:T(8,128)S(1)}, f32[2,128,256]{2,1,0:T(8,128)S(1)}, u32[]{:S(2)}, u32[]{:S(2)}) %collective-permute-start.8) | collective-permute-done | bytes 262176 | tf_op jit(solution)/shard_map/ppermute | solution.py:19
  120.0 1.9 %collective-permute-start.9 = (f32[2,128,256]{2,1,0:T(8,128)S(1)}, f32[2,128,256]{2,1,0:T(8,128)S(1)}, u32[]{:S(2)}, u32[]{:S(2)}) collective-permute-start(f32[2,128,256]{2,1,0:T(8,128)S(1)} %convolution_add_fusion.4), channel_id=1, source_target_pairs={{0,4},{4,8},{8,12},{12,16},{16,20},{20,24},{24,28},{28,32},{32,36}... | collective-permute-start | bytes 786440 | tf_op jit(solution)/shard_map/ppermute | solution.py:19
  121.9 7.9 %collective-permute-done.9 = f32[2,128,256]{2,1,0:T(8,128)S(1)} collective-permute-done((f32[2,128,256]{2,1,0:T(8,128)S(1)}, f32[2,128,256]{2,1,0:T(8,128)S(1)}, u32[]{:S(2)}, u32[]{:S(2)}) %collective-permute-start.9) | collective-permute-done | bytes 262176 | tf_op jit(solution)/shard_map/ppermute | solution.py:19
  130.2 1.9 %collective-permute-start.10 = (f32[2,128,256]{2,1,0:T(8,128)S(1)}, f32[2,128,256]{2,1,0:T(8,128)S(1)}, u32[]{:S(2)}, u32[]{:S(2)}) collective-permute-start(f32[2,128,256]{2,1,0:T(8,128)S(1)} %convolution_add_fusion.3), channel_id=1, source_target_pairs={{0,4},{4,8},{8,12},{12,16},{16,20},{20,24},{24,28},{28,32},{32,36}... | collective-permute-start | bytes 786440 | tf_op jit(solution)/shard_map/ppermute | solution.py:19
  132.1 7.9 %collective-permute-done.10 = f32[2,128,256]{2,1,0:T(8,128)S(1)} collective-permute-done((f32[2,128,256]{2,1,0:T(8,128)S(1)}, f32[2,128,256]{2,1,0:T(8,128)S(1)}, u32[]{:S(2)}, u32[]{:S(2)}) %collective-permute-start.10) | collective-permute-done | bytes 262176 | tf_op jit(solution)/shard_map/ppermute | solution.py:19
  140.4 1.9 %collective-permute-start.11 = (f32[2,128,256]{2,1,0:T(8,128)S(1)}, f32[2,128,256]{2,1,0:T(8,128)S(1)}, u32[]{:S(2)}, u32[]{:S(2)}) collective-permute-start(f32[2,128,256]{2,1,0:T(8,128)S(1)} %convolution_add_fusion.2), channel_id=1, source_target_pairs={{0,4},{4,8},{8,12},{12,16},{16,20},{20,24},{24,28},{28,32},{32,36}... | collective-permute-start | bytes 786440 | tf_op jit(solution)/shard_map/ppermute | solution.py:19
  142.3 7.8 %collective-permute-done.11 = f32[2,128,256]{2,1,0:T(8,128)S(1)} collective-permute-done((f32[2,128,256]{2,1,0:T(8,128)S(1)}, f32[2,128,256]{2,1,0:T(8,128)S(1)}, u32[]{:S(2)}, u32[]{:S(2)}) %collective-permute-start.11) | collective-permute-done | bytes 262176 | tf_op jit(solution)/shard_map/ppermute | solution.py:19
  151.3 0.9 copy-done.2
  152.1 0.7 fusion.49
  (132 shorter events, 15.1 us)
Async XLA Ops:
  0.0 15.9 %copy-start = (bf16[128,512]{1,0:T(8,128)(2,1)S(1)}, bf16[128,512]{1,0:T(8,128)(2,1)}, u32[]{:S(2)}) copy-start(bf16[128,512]{1,0:T(8,128)(2,1)} %param.15) | copy-start | bytes 393220
  0.8 26.7 %collective-permute-start = (bf16[3]{0:T(256)(128)(2,1)S(1)}, bf16[3]{0:T(256)(128)(2,1)S(1)}, u32[]{:S(2)}, u32[]{:S(2)}) collective-permute-start(bf16[3]{0:T(256)(128)(2,1)S(1)} %add_convert_fusion), channel_id=1, source_target_pairs={{0,4},{4,8},{8,12},{12,16},{16,20},{20,24},{24,28},{28,32},{32,36}... | collective-permute-start | bytes 26 | tf_op jit(solution)/shard_map/ppermute | solution.py:19
  3.4 25.8 %collective-permute-start.1 = (bf16[3,256]{1,0:T(4,128)(2,1)S(1)}, bf16[3,256]{1,0:T(4,128)(2,1)S(1)}, u32[]{:S(2)}, u32[]{:S(2)}) collective-permute-start(bf16[3,256]{1,0:T(4,128)(2,1)S(1)} %slice.134), channel_id=1, source_target_pairs={{0,4},{4,8},{8,12},{12,16},{16,20},{20,24},{24,28},{28,32},{32,36}... | collective-permute-start | bytes 4616 | tf_op jit(solution)/shard_map/ppermute | solution.py:19
  8.0 21.2 %collective-permute-start.3 = (bf16[3,256]{1,0:T(4,128)(2,1)S(1)}, bf16[3,256]{1,0:T(4,128)(2,1)S(1)}, u32[]{:S(2)}, u32[]{:S(2)}) collective-permute-start(bf16[3,256]{1,0:T(4,128)(2,1)S(1)} %slice.154), channel_id=1, source_target_pairs={{0,4},{4,8},{8,12},{12,16},{16,20},{20,24},{24,28},{28,32},{32,36}... | collective-permute-start | bytes 4616 | tf_op jit(solution)/shard_map/ppermute | solution.py:19
  10.6 20.4 %collective-permute-start.2 = (bf16[3,512]{1,0:T(4,128)(2,1)S(1)}, bf16[3,512]{1,0:T(4,128)(2,1)S(1)}, u32[]{:S(2)}, u32[]{:S(2)}) collective-permute-start(bf16[3,512]{1,0:T(4,128)(2,1)S(1)} %slice.145), channel_id=1, source_target_pairs={{0,4},{4,8},{8,12},{12,16},{16,20},{20,24},{24,28},{28,32},{32,36}... | collective-permute-start | bytes 9224 | tf_op jit(solution)/shard_map/ppermute | solution.py:19
  14.6 0.7 copy-start.9
  14.6 0.7 copy-start.7
  15.2 0.7 copy-start.8
  15.3 0.7 copy-start.5
  16.0 11.1 %copy-start.11 = (f32[2]{0:T(128)S(1)}, f32[2]{0:T(128)}, u32[]{:S(2)}) copy-start(f32[2]{0:T(128)} %param.24) | copy-start | bytes 28
  16.0 11.1 %copy-start.10 = (f32[2]{0:T(128)S(1)}, f32[2]{0:T(128)}, u32[]{:S(2)}) copy-start(f32[2]{0:T(128)} %param.25) | copy-start | bytes 28
  16.0 11.4 %copy-start.6 = (bf16[4,512]{1,0:T(4,128)(2,1)S(1)}, bf16[4,512]{1,0:T(4,128)(2,1)}, u32[]{:S(2)}) copy-start(bf16[4,512]{1,0:T(4,128)(2,1)} %param.22) | copy-start | bytes 12292
  16.2 13.0 %copy-start.3 = (bf16[128,256]{1,0:T(8,128)(2,1)S(1)}, bf16[128,256]{1,0:T(8,128)(2,1)}, u32[]{:S(2)}) copy-start(bf16[128,256]{1,0:T(8,128)(2,1)} %param.17) | copy-start | bytes 196612
  29.2 0.8 copy-start.4
  30.9 0.9 copy-start.1
  69.1 9.8 %collective-permute-start.4 = (f32[2,128,256]{2,1,0:T(8,128)S(1)}, f32[2,128,256]{2,1,0:T(8,128)S(1)}, u32[]{:S(2)}, u32[]{:S(2)}) collective-permute-start(f32[2,128,256]{2,1,0:T(8,128)S(1)} %convolution_add_fusion.9), channel_id=1, source_target_pairs={{0,4},{4,8},{8,12},{12,16},{16,20},{20,24},{24,28},{28,32},{32,36}... | collective-permute-start | bytes 786440 | tf_op jit(solution)/shard_map/ppermute | solution.py:19
  79.3 9.8 %collective-permute-start.5 = (f32[2,128,256]{2,1,0:T(8,128)S(1)}, f32[2,128,256]{2,1,0:T(8,128)S(1)}, u32[]{:S(2)}, u32[]{:S(2)}) collective-permute-start(f32[2,128,256]{2,1,0:T(8,128)S(1)} %convolution_add_fusion.8), channel_id=1, source_target_pairs={{0,4},{4,8},{8,12},{12,16},{16,20},{20,24},{24,28},{28,32},{32,36}... | collective-permute-start | bytes 786440 | tf_op jit(solution)/shard_map/ppermute | solution.py:19
  89.5 9.8 %collective-permute-start.6 = (f32[2,128,256]{2,1,0:T(8,128)S(1)}, f32[2,128,256]{2,1,0:T(8,128)S(1)}, u32[]{:S(2)}, u32[]{:S(2)}) collective-permute-start(f32[2,128,256]{2,1,0:T(8,128)S(1)} %convolution_add_fusion.7), channel_id=1, source_target_pairs={{0,4},{4,8},{8,12},{12,16},{16,20},{20,24},{24,28},{28,32},{32,36}... | collective-permute-start | bytes 786440 | tf_op jit(solution)/shard_map/ppermute | solution.py:19
  99.6 9.8 %collective-permute-start.7 = (f32[2,128,256]{2,1,0:T(8,128)S(1)}, f32[2,128,256]{2,1,0:T(8,128)S(1)}, u32[]{:S(2)}, u32[]{:S(2)}) collective-permute-start(f32[2,128,256]{2,1,0:T(8,128)S(1)} %convolution_add_fusion.6), channel_id=1, source_target_pairs={{0,4},{4,8},{8,12},{12,16},{16,20},{20,24},{24,28},{28,32},{32,36}... | collective-permute-start | bytes 786440 | tf_op jit(solution)/shard_map/ppermute | solution.py:19
  109.8 9.8 %collective-permute-start.8 = (f32[2,128,256]{2,1,0:T(8,128)S(1)}, f32[2,128,256]{2,1,0:T(8,128)S(1)}, u32[]{:S(2)}, u32[]{:S(2)}) collective-permute-start(f32[2,128,256]{2,1,0:T(8,128)S(1)} %convolution_add_fusion.5), channel_id=1, source_target_pairs={{0,4},{4,8},{8,12},{12,16},{16,20},{20,24},{24,28},{28,32},{32,36}... | collective-permute-start | bytes 786440 | tf_op jit(solution)/shard_map/ppermute | solution.py:19
  120.0 9.8 %collective-permute-start.9 = (f32[2,128,256]{2,1,0:T(8,128)S(1)}, f32[2,128,256]{2,1,0:T(8,128)S(1)}, u32[]{:S(2)}, u32[]{:S(2)}) collective-permute-start(f32[2,128,256]{2,1,0:T(8,128)S(1)} %convolution_add_fusion.4), channel_id=1, source_target_pairs={{0,4},{4,8},{8,12},{12,16},{16,20},{20,24},{24,28},{28,32},{32,36}... | collective-permute-start | bytes 786440 | tf_op jit(solution)/shard_map/ppermute | solution.py:19
  130.2 12.1 %copy-start.12 = (bf16[256]{0:T(256)(128)(2,1)S(1)}, bf16[256]{0:T(256)(128)(2,1)}, u32[]{:S(2)}) copy-start(bf16[256]{0:T(256)(128)(2,1)} %param.26) | copy-start | bytes 1540
  130.2 9.8 %collective-permute-start.10 = (f32[2,128,256]{2,1,0:T(8,128)S(1)}, f32[2,128,256]{2,1,0:T(8,128)S(1)}, u32[]{:S(2)}, u32[]{:S(2)}) collective-permute-start(f32[2,128,256]{2,1,0:T(8,128)S(1)} %convolution_add_fusion.3), channel_id=1, source_target_pairs={{0,4},{4,8},{8,12},{12,16},{16,20},{20,24},{24,28},{28,32},{32,36}... | collective-permute-start | bytes 786440 | tf_op jit(solution)/shard_map/ppermute | solution.py:19
  140.4 9.8 %collective-permute-start.11 = (f32[2,128,256]{2,1,0:T(8,128)S(1)}, f32[2,128,256]{2,1,0:T(8,128)S(1)}, u32[]{:S(2)}, u32[]{:S(2)}) collective-permute-start(f32[2,128,256]{2,1,0:T(8,128)S(1)} %convolution_add_fusion.2), channel_id=1, source_target_pairs={{0,4},{4,8},{8,12},{12,16},{16,20},{20,24},{24,28},{28,32},{32,36}... | collective-permute-start | bytes 786440 | tf_op jit(solution)/shard_map/ppermute | solution.py:19
  151.2 0.9 copy-start.2
where the time goes:
time: 154 us; the launch traced here: 153 us
  waiting for transfers between devices  62.9 us (41%)
  other arithmetic  27.8 us (18%)
  starting transfers between devices  27 us (18%)
  local copies, waits for them, and re-layouts  12.9 us (8%)
  blocking collectives  11 us (7%)
  matrix products  10.3 us (7%)
    ppermute x12, waiting for transfers between devices, passed_along(): return lax.ppermute(value, axis, pairs)  62.9 us
    ppermute x12, starting transfers between devices, passed_along(): return lax.ppermute(value, axis, pairs)  27 us
    another operation x2, other arithmetic, block_terms(): lax.linalg.triangular_solve(system, jnp.transpose(right_side, (1, 0, 2)),...  19.7 us
    psum x1, blocking collectives, local(): gate_total = lax.psum(partial_value, 'tp')  11 us
    dot_general x29, matrix products, product(): return jnp.einsum(pattern, first_op, second_op, precision=highest)  9.42 us
    unnamed x30, local copies, waits for them, and re-layouts  3.85 us
  transfers between devices with their start and end apart: 12, of which 8 were waited for; matrix products, arithmetic and copies ran while one was open for 3% of the time, Pallas kernels for 0%

commit v1 on v0

--- a/solution.py
+++ b/solution.py
@@ -1,6 +1,10 @@
+import functools
+
 import jax
 import jax.numpy as jnp
 from jax import lax
+from jax.experimental import pallas as pl
+from jax.experimental.pallas import tpu as pltpu
 from jax.sharding import PartitionSpec as P
 
 HEADS = 8
@@ -85,6 +89,110 @@
     gating = jax.nn.silu(z_part.astype(jnp.float32).reshape(outputs.shape))
     result = outputs * scale * norm_gain.astype(jnp.float32)[None, None, :] * gating
     return result.astype(jnp.bfloat16).reshape(outputs.shape[0], -1)
+
+
+MESH = pl.DeviceIdType.MESH
+SHIFTS = (1, 2, 4, 1)
+
+
+def fold(high, low):
+    return jnp.dot(high, low, precision=highest, preferred_element_type=jnp.float32)
+
+
+def chain_kernel(
+    devices, carry_ref, inject_ref, out_ref,
+    got_a1, got_b1, got_a2, got_b2, got_b3,
+    own_a2, own_b2, own_a4, own_b4, own_b8,
+    send_sems, recv_sems,
+):
+    me = lax.axis_index("req")
+    tp_me = lax.axis_index("tp")
+    heads = carry_ref.shape[0]
+
+    barrier = pltpu.get_barrier_semaphore()
+    for shift in (1, 2, 4):
+        for peer in (me + shift, me - shift):
+            pl.semaphore_signal(
+                barrier, inc=1, device_id=(lax.rem(peer + devices, devices), tp_me),
+                device_id_type=MESH,
+            )
+    pl.semaphore_wait(barrier, 6)
+
+    def exchange(round_index, sources, targets):
+        shift = SHIFTS[round_index]
+        copies = []
+        for slot, (src, dst) in enumerate(zip(sources, targets)):
+            copies.append(
+                pltpu.make_async_remote_copy(
+                    src_ref=src,
+                    dst_ref=dst,
+                    send_sem=send_sems.at[round_index, slot],
+                    recv_sem=recv_sems.at[round_index, slot],
+                    device_id=(lax.rem(me + shift, devices), tp_me),
+                    device_id_type=MESH,
+                )
+            )
+
+        @pl.when(me + shift < devices)
+        def _():
+            for copy in copies:
+                copy.start()
+
+        @pl.when(me >= shift)
+        def _():
+            for copy in copies:
+                copy.wait_recv()
+
+        @pl.when(me < shift)
+        def _():
+            for dst in targets:
+                dst[...] = jnp.zeros(dst.shape, dst.dtype)
+
+        return copies
+
+    def finish_sends(round_index, copies):
+        shift = SHIFTS[round_index]
+
+        @pl.when(me + shift < devices)
+        def _():
+            for copy in copies:
+                copy.wait_send()
+
+    sent = exchange(0, (carry_ref, inject_ref), (got_a1, got_b1))
+    for h in range(heads):
+        own_a2[h] = fold(carry_ref[h], got_a1[h])
+        own_b2[h] = fold(carry_ref[h], got_b1[h]) + inject_ref[h]
+    finish_sends(0, sent)
+    sent = exchange(1, (own_a2, own_b2), (got_a2, got_b2))
+    for h in range(heads):
+        own_a4[h] = fold(own_a2[h], got_a2[h])
+        own_b4[h] = fold(own_a2[h], got_b2[h]) + own_b2[h]
+    finish_sends(1, sent)
+    sent = exchange(2, (own_b4,), (got_b3,))
+    for h in range(heads):
+        own_b8[h] = fold(own_a4[h], got_b3[h]) + own_b4[h]
+    finish_sends(2, sent)
+    sent = exchange(3, (own_b8,), (out_ref,))
+    finish_sends(3, sent)
+
+
+def carried_in(carry_total, inject_total, devices):
+    heads, dk, dv = inject_total.shape
+    a_shape = pltpu.VMEM((heads, dk, dk), jnp.float32)
+    b_shape = pltpu.VMEM((heads, dk, dv), jnp.float32)
+    return pl.pallas_call(
+        functools.partial(chain_kernel, devices),
+        out_shape=jax.ShapeDtypeStruct((heads, dk, dv), jnp.float32),
+        in_specs=[pl.BlockSpec(memory_space=pltpu.VMEM)] * 2,
+        out_specs=pl.BlockSpec(memory_space=pltpu.VMEM),
+        scratch_shapes=[
+            a_shape, b_shape, a_shape, b_shape, b_shape,
+            a_shape, b_shape, a_shape, b_shape, b_shape,
+            pltpu.SemaphoreType.DMA((4, 2)),
+            pltpu.SemaphoreType.DMA((4, 2)),
+        ],
+        compiler_params=pltpu.CompilerParams(collective_id=0, has_side_effects=True),
+    )(carry_total, inject_total)
 
 
 def local(
@@ -105,18 +213,22 @@
     row_count = q_in.shape[0]
     local_heads = q_in.shape[1] // DK
     edge_rows = CONV - 1
-    seg_marks = (segment_ids[row_count - edge_rows :] + 1).astype(jnp.bfloat16)
-    prior_q, prior_k, prior_v, prior_marks = passed_along(
-        (
+    seg_marks = (segment_ids[row_count - edge_rows :] + 1).astype(jnp.bfloat16)[:, None]
+    q_width, k_width = q_in.shape[1], k_in.shape[1]
+    edges = jnp.concatenate(
+        [
             q_in[row_count - edge_rows :],
             k_in[row_count - edge_rows :],
             v_in[row_count - edge_rows :],
             seg_marks,
-        ),
-        "req",
-        1,
-    )
-    prior_seg = prior_marks.astype(jnp.int32) - 1
+        ],
+        axis=1,
+    )
+    prior = passed_along(edges, "req", 1)
+    prior_q = prior[:, :q_width]
+    prior_k = prior[:, q_width : q_width + k_width]
+    prior_v = prior[:, q_width + k_width : -1]
+    prior_seg = prior[:, -1].astype(jnp.int32) - 1
     seg_ext = jnp.concatenate([prior_seg, segment_ids])
     queries = short_conv(
         jnp.concatenate([prior_q, q_in]).astype(jnp.float32), seg_ext, conv_q, row_count
@@ -137,49 +249,18 @@
     beta_in = lax.dynamic_slice_in_dim(gate_total, HEADS + head_start, local_heads, 1)
     log_alpha = -decay_rate[None, :] * jax.nn.softplus(decay_in + dt_bias[None, :])
     beta_gate = jax.nn.sigmoid(beta_in)
-    block_count = row_count // BLOCK
-    previous = jnp.concatenate([prior_seg[edge_rows - 1 :], segment_ids[:-1]])
-    seg_starts = previous.reshape(block_count, BLOCK)[:, 0]
-
-    def blocks(array):
-        return array.reshape((block_count, BLOCK) + array.shape[1:])
-
-    def sweep_block(running, block_data):
-        carry_acc, inject_acc = running
-        q_part, k_part, v_part, alpha_part, beta_part, seg_part, seg_before = block_data
-        local_out, reach_back, carry_map, injected = block_terms(
-            q_part, k_part, v_part, alpha_part, beta_part, seg_part, seg_before
-        )
-        own_out = local_out + product("hcd,hde->hce", reach_back, inject_acc)
-        lead_map = product("hcd,hde->hce", reach_back, carry_acc)
-        next_running = (
-            product("hde,hef->hdf", carry_map, carry_acc),
-            product("hde,hef->hdf", carry_map, inject_acc) + injected,
-        )
-        return (next_running, (own_out, lead_map))
-
-    identity = jnp.broadcast_to(jnp.eye(DK, dtype=jnp.float32), (local_heads, DK, DK))
-    empty = jnp.zeros((local_heads, DK, DV), jnp.float32)
-    block_data = (
-        blocks(queries.reshape(row_count, local_heads, DK)),
-        blocks(keyset),
-        blocks(values.reshape(row_count, local_heads, DV)),
-        blocks(log_alpha),
-        blocks(beta_gate),
-        blocks(segment_ids),
-        seg_starts,
-    )
-    totals, outputs = lax.scan(sweep_block, (identity, empty), block_data)
-    carry_total, inject_total = totals
-    own_out, lead_map = outputs
-    span = min(8, lax.axis_size("req") // 2)
-    incoming = empty
-    for hop_index in range(span):
-        incoming = passed_along(
-            product("hde,hef->hdf", carry_total, incoming) + inject_total, "req", 1
-        )
-    head_out = own_out + product("nhcd,hde->nhce", lead_map, incoming)
-    head_out = jnp.transpose(head_out, (0, 2, 1, 3)).reshape(row_count, local_heads, DV)
+    local_out, reach_back, carry_map, injected = block_terms(
+        queries.reshape(row_count, local_heads, DK),
+        keyset,
+        values.reshape(row_count, local_heads, DV),
+        log_alpha,
+        beta_gate,
+        segment_ids,
+        prior_seg[edge_rows - 1],
+    )
+    incoming = carried_in(carry_map, injected, lax.axis_size("req"))
+    head_out = local_out + product("hcd,hde->hce", reach_back, incoming)
+    head_out = jnp.transpose(head_out, (1, 0, 2))
     return finish(head_out, z_in, norm_gain)
 
 

time: 154 us -> 100 us (0.65)
  the two profiles are of different devices: /device:TPU:6 before, /device:TPU:128 now
where the time goes in v1:
time: 100 us; the launch traced here: 99.6 us
  Pallas kernels  44.5 us (44%)
  other arithmetic  24.2 us (24%)
  local copies, waits for them, and re-layouts  12.6 us (13%)
  blocking collectives  11 us (11%)
  matrix products  5.02 us (5%)
  starting transfers between devices  1.92 us (2%)
    pallas_call x1, Pallas kernels, carried_in(): pl.pallas_call(functools.partial(chain_kernel, devices), out_shape=jax.Sh...  44.5 us
    another operation x1, other arithmetic, block_terms(): lax.linalg.triangular_solve(system, jnp.transpose(right_side, (1, 0, 2)),...  19.7 us
    psum x1, blocking collectives, local(): gate_total = lax.psum(partial_value, 'tp')  11 us
    unnamed x32, local copies, waits for them, and re-layouts  7.97 us
    dot_general x7, matrix products, product(): return jnp.einsum(pattern, first_op, second_op, precision=highest)  4.36 us
  transfers between devices with their start and end apart: 1, of which 0 were waited for; matrix products, arithmetic and copies ran while one was open for 2% of the time, Pallas kernels for 0%

profile of v1, /device:TPU:128, one launch (start us, length us, event | category | flops | bytes accessed | tf_op | source)
XLA Modules:
  0.0 99.6 jit_solution(6927352618186062252)
XLA Ops:
  0.0 0.7 slice.137
  0.7 0.2 copy.92
  0.9 0.7 copy-done.4
  1.6 0.1 copy.90
  1.7 0.7 copy-done.5
  2.4 0.1 copy.91
  2.6 0.5 copy-done.10
  3.2 1.9 %collective-permute-start = (bf16[3,1025]{0,1:T(8,128)(2,1)S(1)}, bf16[3,1025]{0,1:T(8,128)(2,1)S(1)}, u32[]{:S(2)}, u32[]{:S(2)}) collective-permute-start(bf16[3,1025]{0,1:T(8,128)(2,1)S(1)} %pad_maximum_fusion), channel_id=1, source_target_pairs={{0,4},{4,8},{8,12},{12,16},{16,20},{20,24},{24,28},{28,32},{32,36}... | collective-permute-start | bytes 18458 | tf_op jit(solution)/shard_map/ppermute | solution.py:23
  5.3 0.6 copy-done.8
  5.8 0.7 copy-done.6
  6.6 0.1 fusion.54
  6.7 11.0 %psum.7 = f32[128,16]{0,1:T(8,128)S(1)} all-reduce(f32[128,16]{0,1:T(8,128)S(1)} %fusion.54), channel_id=1, replica_groups=mesh['req'=128,'tp'=4] {'tp'}, use_global_device_ids=true, to_apply=%region_1.2 | all-reduce | flops 2048 | bytes 16384 | tf_op jit(solution)/shard_map/psum | solution.py:246
  17.7 0.6 copy-done.11
  18.4 0.1 copy.97
  18.6 0.6 copy-done.7
  19.2 0.2 reduce_window_sum.11
  19.3 0.5 copy-done.9
  19.9 0.6 slice.175
  20.7 0.7 copy-done.2
  21.5 0.1 copy.101
  21.7 0.7 copy-done.3
  22.4 0.1 copy.109
  22.5 0.1 copy.111
  22.6 0.5 copy-done.13
  23.2 0.6 slice.170
  23.9 1.3 %compare_convert_fusion = (f32[128]{0:T(128)S(1)}, f32[128]{0:T(128)S(1)}, pred[128]{0:T(512)(128)(4,1)S(1)}, pred[128]{0:T(512)(128)(4,1)S(1)}, pred[128]{0:T(512)(128)(4,1)S(1)}) fusion(s32[128]{0:T(128)S(1)} %copy-done.10, s32[]{:T(128)} %bitcast.27, s32[]{:T(128)} %bitcast.22, s32[131]{0:T(256)S(1)} %pad_add_fusion), kind=kLoop, calls=%fused_computation.90 | loop fusion | flops 896 | bytes 3464 | tf_op jit(solution)/shard_map/convert_element_type | solution.py:57
  25.2 0.1 maximum_convert_fusion.1
  25.4 0.3 multiply_reduce_fusion.1
  25.8 0.6 slice.173
  26.4 0.3 divide_multiply_fusion.2
  26.9 0.4 convolution_multiply_fusion.1
  27.3 0.5 fusion.4
  27.8 19.7 %custom-call.3 = f32[2,1,128,128]{2,3,1,0:T(8,128)S(1)} custom-call(f32[2,1,128,128]{3,2,1,0:T(8,128)S(1)} %fusion.4), custom_call_target="InvertDiagBlocksLowerTriangular" | custom-call | tf_op jit(solution)/shard_map/triangular_solve | solution.py:67
  47.5 0.1 multiply_multiply_fusion
  47.6 0.1 maximum_convert_fusion
  47.8 0.6 divide_multiply_fusion
  48.4 0.1 copy.102
  48.8 0.7 exponential_multiply_fusion.2
  49.4 0.5 fusion.5
  50.0 1.2 %fusion.14.inject_ref = f32[2,128,256]{2,1,0:T(8,128)} fusion(f32[2,128,384]{2,1,0:T(8,128)S(1)} %fusion.5, f32[128,2,128]{2,0,1:T(8,128)S(1)} %copy.95, f32[128,2]{0,1:T(2,128)S(1)} %copy.106, f32[128,2]{0,1:T(2,128)S(1)} %add_rsqrt_fusion.1), kind=kOutput, calls=%fused_computation.29 | convolution fusion | flops 100728832 | bytes 657408 | tf_op jit(solution)/shard_map/hcd,hce->hde/dot_general | solution.py:27
  51.2 1.1 %convolution_subtract_fusion.carry_ref = f32[2,128,128]{2,1,0:T(8,128)} fusion(f32[2,128,384]{2,1,0:T(8,128)S(1)} %fusion.5, f32[128,2,128]{2,0,1:T(8,128)S(1)} %copy.95, f32[128,2]{0,1:T(2,128)S(1)} %copy.106, f32[2]{0:T(128)S(1)} %exponential_multiply_fusion.2, f32[128,128]{1,0:T(8,128)S(1)} %get-tuple-element.41, f32[128,2]{0,1:T(2,128)S(1)} %add_rsqrt_fusion.1), kind=kOutput, calls=%fused_computation.2 | convolution fusion | flops 50462720 | bytes 461312 | tf_op jit(solution)/shard_map/hcd,hce->hde/dot_general | solution.py:27
  52.3 0.4 fusion.16
  52.7 44.5 %shard_map.127 = f32[2,128,256]{2,1,0:T(8,128)} custom-call(f32[2,128,128]{2,1,0:T(8,128)} %convolution_subtract_fusion.carry_ref, f32[2,128,256]{2,1,0:T(8,128)} %fusion.14.inject_ref), custom_call_target="tpu_custom_call" | custom-call | tf_op jit(solution)/shard_map/pallas_call | solution.py:183
  97.2 0.3 convolution_subtract_fusion.1
  97.5 0.7 copy-done.1
  98.1 0.4 multiply_reduce_fusion
  98.7 0.1 copy.112
  98.8 0.8 copy.113
  (47 shorter events, 1.4 us)
Async XLA Ops:
  0.0 5.8 %copy-start = (bf16[128,512]{1,0:T(8,128)(2,1)S(1)}, bf16[128,512]{1,0:T(8,128)(2,1)}, u32[]{:S(2)}) copy-start(bf16[128,512]{1,0:T(8,128)(2,1)} %param.13) | copy-start | bytes 393220
  0.7 0.8 copy-start.4
  1.6 0.8 copy-start.5
  2.4 0.7 copy-start.10
  3.2 19.9 %collective-permute-start = (bf16[3,1025]{0,1:T(8,128)(2,1)S(1)}, bf16[3,1025]{0,1:T(8,128)(2,1)S(1)}, u32[]{:S(2)}, u32[]{:S(2)}) collective-permute-start(bf16[3,1025]{0,1:T(8,128)(2,1)S(1)} %pad_maximum_fusion), channel_id=1, source_target_pairs={{0,4},{4,8},{8,12},{12,16},{16,20},{20,24},{24,28},{28,32},{32,36}... | collective-permute-start | bytes 18458 | tf_op jit(solution)/shard_map/ppermute | solution.py:23
  5.2 0.7 copy-start.8
  5.8 0.7 copy-start.6
  6.7 11.0 %copy-start.12 = (f32[2]{0:T(128)S(1)}, f32[2]{0:T(128)}, u32[]{:S(2)}) copy-start(f32[2]{0:T(128)} %param.22) | copy-start | bytes 28
  17.7 0.7 copy-start.11
  18.4 0.7 copy-start.7
  19.1 0.7 copy-start.9
  20.6 0.9 copy-start.2
  21.5 0.9 copy-start.3
  22.5 0.7 copy-start.13
  97.2 1.0 copy-start.1

commit v2 on v1

--- a/solution.py
+++ b/solution.py
@@ -59,14 +59,11 @@
     coupling = (
         jnp.transpose(beta_gate)[:, :, None] * key_dots * jnp.where(strict[None], decays, 0.0)
     )
-    system = jnp.eye(length, dtype=jnp.float32)[None] + coupling
     start_scale = jnp.exp(cumulative) * linked[:, None]
     right_side = jnp.concatenate(
         [beta_gate[:, :, None] * values, (beta_gate * start_scale)[:, :, None] * keyset], axis=2
     )
-    solved = lax.linalg.triangular_solve(
-        system, jnp.transpose(right_side, (1, 0, 2)), left_side=True, lower=True
-    )
+    solved = unit_lower_solve(coupling, jnp.transpose(right_side, (1, 0, 2)))
     fresh_part = solved[:, :, :width]
     carried = solved[:, :, width:]
     scores = product("ihd,jhd->hij", queries, keyset) * decays
@@ -92,7 +89,6 @@
 
 
 MESH = pl.DeviceIdType.MESH
-SHIFTS = (1, 2, 4, 1)
 
 
 def fold(high, low):
@@ -101,37 +97,32 @@
 
 def chain_kernel(
     devices, carry_ref, inject_ref, out_ref,
-    got_a1, got_b1, got_a2, got_b2, got_b3,
-    own_a2, own_b2, own_a4, own_b4, own_b8,
+    got1_a, got1_b, got2_a, got2_b, got3_b, got4_b,
+    lo_a, lo_b, join_a, join_b, pair_a, pair_b, quad_b, reply,
     send_sems, recv_sems,
 ):
     me = lax.axis_index("req")
     tp_me = lax.axis_index("tp")
-    heads = carry_ref.shape[0]
+    core = lax.rem(me, 2)
+    partner = me + 1 - 2 * core
+
+    def at(device):
+        return (lax.rem(device + devices, devices), tp_me)
 
     barrier = pltpu.get_barrier_semaphore()
-    for shift in (1, 2, 4):
-        for peer in (me + shift, me - shift):
-            pl.semaphore_signal(
-                barrier, inc=1, device_id=(lax.rem(peer + devices, devices), tp_me),
-                device_id_type=MESH,
-            )
-    pl.semaphore_wait(barrier, 6)
-
-    def exchange(round_index, sources, targets):
-        shift = SHIFTS[round_index]
-        copies = []
-        for slot, (src, dst) in enumerate(zip(sources, targets)):
-            copies.append(
-                pltpu.make_async_remote_copy(
-                    src_ref=src,
-                    dst_ref=dst,
-                    send_sem=send_sems.at[round_index, slot],
-                    recv_sem=recv_sems.at[round_index, slot],
-                    device_id=(lax.rem(me + shift, devices), tp_me),
-                    device_id_type=MESH,
-                )
-            )
+    for peer in (partner, me + 2, me - 2, me + 4, me - 4):
+        pl.semaphore_signal(barrier, inc=1, device_id=at(peer), device_id_type=MESH)
+    pl.semaphore_wait(barrier, 5)
+
+    def remote(step, slot, src, dst, target):
+        return pltpu.make_async_remote_copy(
+            src_ref=src, dst_ref=dst,
+            send_sem=send_sems.at[step, slot], recv_sem=recv_sems.at[step, slot],
+            device_id=at(target), device_id_type=MESH,
+        )
+
+    def along(step, pairs, shift):
+        copies = [remote(step, slot, src, dst, me + shift) for slot, (src, dst) in enumerate(pairs)]
 
         @pl.when(me + shift < devices)
         def _():
@@ -145,54 +136,101 @@
 
         @pl.when(me < shift)
         def _():
-            for dst in targets:
+            for _, dst in pairs:
                 dst[...] = jnp.zeros(dst.shape, dst.dtype)
 
         return copies
 
-    def finish_sends(round_index, copies):
-        shift = SHIFTS[round_index]
-
+    def sent(copies, shift):
         @pl.when(me + shift < devices)
         def _():
             for copy in copies:
                 copy.wait_send()
 
-    sent = exchange(0, (carry_ref, inject_ref), (got_a1, got_b1))
-    for h in range(heads):
-        own_a2[h] = fold(carry_ref[h], got_a1[h])
-        own_b2[h] = fold(carry_ref[h], got_b1[h]) + inject_ref[h]
-    finish_sends(0, sent)
-    sent = exchange(1, (own_a2, own_b2), (got_a2, got_b2))
-    for h in range(heads):
-        own_a4[h] = fold(own_a2[h], got_a2[h])
-        own_b4[h] = fold(own_a2[h], got_b2[h]) + own_b2[h]
-    finish_sends(1, sent)
-    sent = exchange(2, (own_b4,), (got_b3,))
-    for h in range(heads):
-        own_b8[h] = fold(own_a4[h], got_b3[h]) + own_b4[h]
-    finish_sends(2, sent)
-    sent = exchange(3, (own_b8,), (out_ref,))
-    finish_sends(3, sent)
+    first = [
+        remote(0, 0, carry_ref.at[1 - core], got1_a, partner),
+        remote(0, 1, inject_ref.at[1 - core], got1_b, partner),
+    ]
+    for copy in first:
+        copy.start()
+    for copy in first:
+        copy.wait_recv()
+    own_a = carry_ref[core]
+    own_b = inject_ref[core]
+    low = core == 0
+    lo_a[...] = jnp.where(low, own_a, got1_a[...])
+    lo_b[...] = jnp.where(low, own_b, got1_b[...])
+    hi_a = jnp.where(low, got1_a[...], own_a)
+    hi_b = jnp.where(low, got1_b[...], own_b)
+    join_a[...] = fold(hi_a, lo_a[...])
+    join_b[...] = fold(hi_a, lo_b[...]) + hi_b
+    for copy in first:
+        copy.wait_send()
+
+    copies = along(1, ((join_a, got2_a), (join_b, got2_b)), 2)
+    pair_a[...] = fold(join_a[...], got2_a[...])
+    pair_b[...] = fold(join_a[...], got2_b[...]) + join_b[...]
+    sent(copies, 2)
+
+    copies = along(2, ((pair_b, got3_b),), 4)
+    quad_b[...] = fold(pair_a[...], got3_b[...]) + pair_b[...]
+    sent(copies, 4)
+
+    copies = along(3, ((quad_b, got4_b),), 2)
+    entering = got4_b[...]
+    onward = fold(lo_a[...], entering) + lo_b[...]
+    sent(copies, 2)
+
+    reply[...] = jnp.where(low, onward, entering)
+    last = remote(4, 0, reply, out_ref.at[core], partner)
+    last.start()
+    out_ref[core] = jnp.where(low, entering, onward)
+    remote(4, 0, reply, out_ref.at[1 - core], partner).wait_recv()
+    last.wait_send()
 
 
 def carried_in(carry_total, inject_total, devices):
     heads, dk, dv = inject_total.shape
-    a_shape = pltpu.VMEM((heads, dk, dk), jnp.float32)
-    b_shape = pltpu.VMEM((heads, dk, dv), jnp.float32)
+    a_shape = pltpu.VMEM((dk, dk), jnp.float32)
+    b_shape = pltpu.VMEM((dk, dv), jnp.float32)
     return pl.pallas_call(
         functools.partial(chain_kernel, devices),
         out_shape=jax.ShapeDtypeStruct((heads, dk, dv), jnp.float32),
         in_specs=[pl.BlockSpec(memory_space=pltpu.VMEM)] * 2,
         out_specs=pl.BlockSpec(memory_space=pltpu.VMEM),
         scratch_shapes=[
-            a_shape, b_shape, a_shape, b_shape, b_shape,
-            a_shape, b_shape, a_shape, b_shape, b_shape,
-            pltpu.SemaphoreType.DMA((4, 2)),
-            pltpu.SemaphoreType.DMA((4, 2)),
+            a_shape, b_shape, a_shape, b_shape, b_shape, b_shape,
+            a_shape, b_shape, a_shape, b_shape, a_shape, b_shape, b_shape, b_shape,
+            pltpu.SemaphoreType.DMA((5, 2)),
+            pltpu.SemaphoreType.DMA((5, 2)),
         ],
         compiler_params=pltpu.CompilerParams(collective_id=0, has_side_effects=True),
     )(carry_total, inject_total)
+
+
+def solve_kernel(coupling_ref, rhs_ref, out_ref):
+    length = coupling_ref.shape[1]
+    rows = lax.broadcasted_iota(jnp.int32, (length, length), 0)
+    cols = lax.broadcasted_iota(jnp.int32, (length, length), 1)
+    eye = (rows == cols).astype(jnp.float32)
+    for h in range(coupling_ref.shape[0]):
+        power = -coupling_ref[h]
+        inverse = eye + power
+        span = 2
+        while span < length:
+            power = fold(power, power)
+            inverse = inverse + fold(inverse, power)
+            span *= 2
+        out_ref[h] = fold(inverse, rhs_ref[h])
+
+
+def unit_lower_solve(coupling, rhs):
+    return pl.pallas_call(
+        solve_kernel,
+        out_shape=jax.ShapeDtypeStruct(rhs.shape, jnp.float32),
+        in_specs=[pl.BlockSpec(memory_space=pltpu.VMEM)] * 2,
+        out_specs=pl.BlockSpec(memory_space=pltpu.VMEM),
+    )(coupling, rhs)
 
 
 def local(

time: 100 us -> 79.9 us (0.80)
  the two profiles are of different devices: /device:TPU:128 before, /device:TPU:7 now
where the time goes in v2:
time: 79.9 us; the launch traced here: 79.3 us
  Pallas kernels  41.4 us (52%)
  local copies, waits for them, and re-layouts  12.7 us (16%)
  blocking collectives  9.26 us (12%)
  matrix products  6.17 us (8%)
  other arithmetic  5.33 us (7%)
  starting transfers between devices  4.11 us (5%)
    pallas_call x1, Pallas kernels, carried_in(): pl.pallas_call(functools.partial(chain_kernel, devices), out_shape=jax.Sh...  35.9 us
    psum x1, blocking collectives, local(): gate_total = lax.psum(partial_value, 'tp')  9.26 us
    unnamed x34, local copies, waits for them, and re-layouts  7.97 us
    dot_general x7, matrix products, product(): return jnp.einsum(pattern, first_op, second_op, precision=highest)  6.04 us
    pallas_call x1, Pallas kernels, unit_lower_solve(): pl.pallas_call(solve_kernel, out_shape=jax.ShapeDtypeStruct(rhs.shape, jn...  5.59 us
    ppermute x1, starting transfers between devices, passed_along(): return lax.ppermute(value, axis, pairs)  4.11 us
  transfers between devices with their start and end apart: 1, of which 0 were waited for; matrix products, arithmetic and copies ran while one was open for 2% of the time, Pallas kernels for 0%

profile of v2, /device:TPU:7, one launch (start us, length us, event | category | flops | bytes accessed | tf_op | source)
XLA Modules:
  0.0 79.3 jit_solution(16882613084324191030)
XLA Ops:
  0.0 0.7 slice.133
  0.7 0.2 copy.84
  0.9 0.7 copy-done.5
  1.6 0.1 copy.82
  1.7 0.7 copy-done.6
  2.4 0.1 copy.83
  2.6 0.5 copy-done.11
  3.2 4.1 %collective-permute-start = (bf16[3,1025]{0,1:T(8,128)(2,1)S(1)}, bf16[3,1025]{0,1:T(8,128)(2,1)S(1)}, u32[]{:S(2)}, u32[]{:S(2)}) collective-permute-start(bf16[3,1025]{0,1:T(8,128)(2,1)S(1)} %pad_maximum_fusion), channel_id=1, source_target_pairs={{0,4},{4,8},{8,12},{12,16},{16,20},{20,24},{24,28},{28,32},{32,36}... | collective-permute-start | bytes 18458 | tf_op jit(solution)/shard_map/ppermute | solution.py:23
  7.4 0.6 copy-done.9
  8.0 0.7 copy-done.7
  8.7 0.1 fusion.46
  8.9 9.3 %psum.7 = f32[128,16]{0,1:T(8,128)S(1)} all-reduce(f32[128,16]{0,1:T(8,128)S(1)} %fusion.46), channel_id=1, replica_groups=mesh['req'=128,'tp'=4] {'tp'}, use_global_device_ids=true, to_apply=%region_1.2 | all-reduce | flops 2048 | bytes 16384 | tf_op jit(solution)/shard_map/psum | solution.py:284
  18.2 0.6 copy-done.12
  18.9 0.1 copy.89
  19.0 0.6 copy-done.8
  19.6 0.2 reduce_window_sum.11
  19.8 0.5 copy-done.10
  20.3 0.6 slice.171
  21.2 0.7 copy-done.3
  21.9 0.1 copy.92
  22.1 0.7 copy-done.4
  22.8 0.1 copy.99
  23.1 0.5 copy-done.14
  23.7 0.6 slice.166
  24.3 1.3 %compare_convert_fusion = (f32[128]{0:T(128)S(1)}, f32[128]{0:T(128)S(1)}, pred[128]{0:T(512)(128)(4,1)S(1)}, pred[128]{0:T(512)(128)(4,1)S(1)}, pred[128]{0:T(512)(128)(4,1)S(1)}) fusion(s32[128]{0:T(128)S(1)} %copy-done.11, s32[]{:T(128)} %bitcast.24, s32[]{:T(128)} %bitcast.19, s32[131]{0:T(256)S(1)} %pad_add_fusion), kind=kLoop, calls=%fused_computation.83 | loop fusion | flops 896 | bytes 3464 | tf_op jit(solution)/shard_map/convert_element_type | solution.py:57
  25.7 0.1 maximum_convert_fusion.1
  25.8 0.3 multiply_reduce_fusion.1
  26.3 0.1 maximum_convert_fusion
  26.5 0.6 divide_multiply_fusion
  27.0 0.1 copy.93
  27.3 0.6 slice.169
  27.9 0.7 exponential_multiply_fusion.2
  28.6 0.3 divide_multiply_fusion.2
  29.1 0.1 multiply_multiply_fusion
  29.3 0.8 maximum_bitcast_fusion.rhs_ref
  30.1 0.4 convolution_multiply_fusion.1
  30.5 1.1 %fusion.1.coupling_ref = f32[2,128,128]{2,1,0:T(8,128)} fusion(f32[128,2,128]{2,0,1:T(8,128)S(1)} %copy.87, f32[2,128]{1,0:T(2,128)S(1)} %bitcast.61, f32[2,128]{1,0:T(2,128)S(1)} %copy.90, f32[128,2]{0,1:T(2,128)S(1)} %add_rsqrt_fusion.1, pred[128,128]{1,0:T(8,128)(4,1)S(1)} %get-tuple-element.34, pred[128,128]{1,0:T(8,128)(4,1)S(1)} %get-tuple-element.35), kind=kOutput, calls=%fused_computation.5 | convolution fusion | flops 50561024 | bytes 297984 | tf_op jit(solution)/shard_map/ihd,jhd->hij/dot_general | solution.py:27
  31.6 5.6 %shard_map.127 = f32[2,128,384]{2,1,0:T(8,128)} custom-call(f32[2,128,128]{2,1,0:T(8,128)} %fusion.1.coupling_ref, f32[2,128,384]{2,1,0:T(8,128)} %maximum_bitcast_fusion.rhs_ref), custom_call_target="tpu_custom_call" | custom-call | tf_op jit(solution)/shard_map/pallas_call | solution.py:228
  37.2 2.2 %fusion.8.inject_ref = f32[2,128,256]{2,1,0:T(8,128)} fusion(f32[2,128,384]{2,1,0:T(8,128)} %shard_map.127, f32[128,2,128]{2,0,1:T(8,128)S(1)} %copy.87, f32[128,2]{0,1:T(2,128)S(1)} %copy.96, f32[128,2]{0,1:T(2,128)S(1)} %add_rsqrt_fusion.1), kind=kOutput, calls=%fused_computation.23 | convolution fusion | flops 100728832 | bytes 657408 | tf_op jit(solution)/shard_map/hcd,hce->hde/dot_general | solution.py:27
  39.5 0.4 fusion.10
  39.9 1.1 %convolution_subtract_fusion.carry_ref = f32[2,128,128]{2,1,0:T(8,128)} fusion(f32[2,128,384]{2,1,0:T(8,128)S(1)} %copy-done.1, f32[128,2,128]{2,0,1:T(8,128)S(1)} %copy.87, f32[128,2]{0,1:T(2,128)S(1)} %copy.96, f32[128,128]{1,0:T(8,128)S(1)} %fusion.40, f32[2]{0:T(128)S(1)} %exponential_multiply_fusion.2, f32[128,2]{0,1:T(2,128)S(1)} %add_rsqrt_fusion.1), kind=kOutput, calls=%fused_computation.2 | convolution fusion | flops 50462720 | bytes 461312 | tf_op jit(solution)/shard_map/hcd,hce->hde/dot_general | solution.py:27
  41.0 35.9 %shard_map.128 = f32[2,128,256]{2,1,0:T(8,128)} custom-call(f32[2,128,128]{2,1,0:T(8,128)} %convolution_subtract_fusion.carry_ref, f32[2,128,256]{2,1,0:T(8,128)} %fusion.8.inject_ref), custom_call_target="tpu_custom_call" | custom-call | tf_op jit(solution)/shard_map/pallas_call | solution.py:196
  76.9 0.3 convolution_subtract_fusion.1
  77.1 0.7 copy-done.2
  77.8 0.5 multiply_reduce_fusion
  78.3 0.1 multiply_convert_fusion
  78.4 0.1 copy.102
  78.5 0.8 copy.103
  (49 shorter events, 1.4 us)
Async XLA Ops:
  0.0 8.0 %copy-start = (bf16[128,512]{1,0:T(8,128)(2,1)S(1)}, bf16[128,512]{1,0:T(8,128)(2,1)}, u32[]{:S(2)}) copy-start(bf16[128,512]{1,0:T(8,128)(2,1)} %param.13) | copy-start | bytes 393220
  0.7 0.8 %copy-start.5 = (bf16[128,256]{1,0:T(8,128)(2,1)S(1)}, bf16[128,256]{1,0:T(8,128)(2,1)}, u32[]{:S(2)}) copy-start(bf16[128,256]{1,0:T(8,128)(2,1)} %param.14) | copy-start | bytes 196612
  1.6 0.8 %copy-start.6 = (bf16[128,256]{1,0:T(8,128)(2,1)S(1)}, bf16[128,256]{1,0:T(8,128)(2,1)}, u32[]{:S(2)}) copy-start(bf16[128,256]{1,0:T(8,128)(2,1)} %param.15) | copy-start | bytes 196612
  2.4 0.7 copy-start.11
  3.2 20.4 %collective-permute-start = (bf16[3,1025]{0,1:T(8,128)(2,1)S(1)}, bf16[3,1025]{0,1:T(8,128)(2,1)S(1)}, u32[]{:S(2)}, u32[]{:S(2)}) collective-permute-start(bf16[3,1025]{0,1:T(8,128)(2,1)S(1)} %pad_maximum_fusion), channel_id=1, source_target_pairs={{0,4},{4,8},{8,12},{12,16},{16,20},{20,24},{24,28},{28,32},{32,36}... | collective-permute-start | bytes 18458 | tf_op jit(solution)/shard_map/ppermute | solution.py:23
  7.3 0.7 copy-start.9
  8.0 0.7 copy-start.7
  8.9 9.3 %copy-start.13 = (f32[2]{0:T(128)S(1)}, f32[2]{0:T(128)}, u32[]{:S(2)}) copy-start(f32[2]{0:T(128)} %param.22) | copy-start | bytes 28
  18.2 0.7 copy-start.12
  18.9 0.7 copy-start.8
  19.6 0.7 copy-start.10
  21.0 0.9 %copy-start.3 = (bf16[128,512]{1,0:T(8,128)(2,1)S(1)}, bf16[128,512]{1,0:T(8,128)(2,1)}, u32[]{:S(2)}) copy-start(bf16[128,512]{1,0:T(8,128)(2,1)} %param.16) | copy-start | bytes 393220
  21.9 0.9 %copy-start.4 = (bf16[128,512]{1,0:T(8,128)(2,1)S(1)}, bf16[128,512]{1,0:T(8,128)(2,1)}, u32[]{:S(2)}) copy-start(bf16[128,512]{1,0:T(8,128)(2,1)} %param.17) | copy-start | bytes 393220
  22.9 0.7 copy-start.14
  37.2 2.3 %copy-start.1 = (f32[2,128,384]{2,1,0:T(8,128)S(1)}, f32[2,128,384]{2,1,0:T(8,128)}, u32[]{:S(2)}) copy-start(f32[2,128,384]{2,1,0:T(8,128)} %shard_map.127) | copy-start | bytes 1179652
  76.9 1.0 %copy-start.2 = (f32[2,128,256]{2,1,0:T(8,128)S(1)}, f32[2,128,256]{2,1,0:T(8,128)}, u32[]{:S(2)}) copy-start(f32[2,128,256]{2,1,0:T(8,128)} %shard_map.128) | copy-start | bytes 786436

commit v3 on v2

--- a/solution.py
+++ b/solution.py
@@ -231,6 +231,68 @@
         in_specs=[pl.BlockSpec(memory_space=pltpu.VMEM)] * 2,
         out_specs=pl.BlockSpec(memory_space=pltpu.VMEM),
     )(coupling, rhs)
+
+
+def gate_kernel(groups, input_ref, weight_ref, out_ref, partial, got, send_sems, recv_sems):
+    me = lax.axis_index("tp")
+    row = lax.axis_index("req")
+    barrier = pltpu.get_barrier_semaphore()
+    for step in range(1, groups):
+        pl.semaphore_signal(
+            barrier, inc=1, device_id=(row, lax.rem(me + step, groups)), device_id_type=MESH
+        )
+    pl.semaphore_wait(barrier, groups - 1)
+    partial[...] = jnp.dot(input_ref[...], weight_ref[...], preferred_element_type=jnp.float32)
+    copies = []
+    for step in range(1, groups):
+        copies.append(
+            pltpu.make_async_remote_copy(
+                src_ref=partial,
+                dst_ref=got.at[me],
+                send_sem=send_sems.at[step],
+                recv_sem=recv_sems.at[me],
+                device_id=(row, lax.rem(me + step, groups)),
+                device_id_type=MESH,
+            )
+        )
+    for copy in copies:
+        copy.start()
+    for source in range(groups):
+
+        @pl.when(source != me)
+        def _():
+            pltpu.make_async_remote_copy(
+                src_ref=partial,
+                dst_ref=got.at[source],
+                send_sem=send_sems.at[0],
+                recv_sem=recv_sems.at[source],
+                device_id=(row, source),
+                device_id_type=MESH,
+            ).wait_recv()
+
+    total = jnp.zeros(out_ref.shape, jnp.float32)
+    for source in range(groups):
+        total = total + jnp.where(source == me, partial[...], got[source])
+    out_ref[...] = total
+    for copy in copies:
+        copy.wait_send()
+
+
+def gate_sum(layer_input, gate_weight, groups):
+    rows, width = layer_input.shape[0], gate_weight.shape[1]
+    return pl.pallas_call(
+        functools.partial(gate_kernel, groups),
+        out_shape=jax.ShapeDtypeStruct((rows, width), jnp.float32),
+        in_specs=[pl.BlockSpec(memory_space=pltpu.VMEM)] * 2,
+        out_specs=pl.BlockSpec(memory_space=pltpu.VMEM),
+        scratch_shapes=[
+            pltpu.VMEM((rows, width), jnp.float32),
+            pltpu.VMEM((groups, rows, width), jnp.float32),
+            pltpu.SemaphoreType.DMA((groups,)),
+            pltpu.SemaphoreType.DMA((groups,)),
+        ],
+        compiler_params=pltpu.CompilerParams(collective_id=1, has_side_effects=True),
+    )(layer_input, gate_weight)
 
 
 def local(
@@ -280,8 +342,7 @@
     values = short_conv(
         jnp.concatenate([prior_v, v_in]).astype(jnp.float32), seg_ext, conv_v, row_count
     )
-    partial_value = jnp.dot(layer_input, gate_weight, preferred_element_type=jnp.float32)
-    gate_total = lax.psum(partial_value, "tp")
+    gate_total = gate_sum(layer_input, gate_weight, lax.axis_size("tp"))
     head_start = lax.axis_index("tp") * local_heads
     decay_in = lax.dynamic_slice_in_dim(gate_total, head_start, local_heads, 1)
     beta_in = lax.dynamic_slice_in_dim(gate_total, HEADS + head_start, local_heads, 1)

time: 79.9 us -> 81.4 us (1.019)
  Pallas kernels: 41.4 us -> 51.2 us
  blocking collectives: 9.26 us -> 0 us
  other arithmetic: 5.33 us -> 6.25 us
    pallas_call x0 -> x1, Pallas kernels: none -> 9.61 us  [gate_sum(): pl.pallas_call(functools.partial(gate_kernel, groups), out_shape=jax.Shap...]
    psum x1 -> x0, blocking collectives: 9.26 us -> none  [local(): gate_total = lax.psum(partial_value, 'tp')]
    mul x1, other arithmetic: 0.08 us -> 0.96 us  [local(): -decay_rate[None, :] * jax.nn.softplus(decay_in + dt_bias[None, :])]
    unnamed x34 -> x35, local copies, waits for them, and re-layouts: 7.97 us -> 8.12 us
  transfers between devices with their start and end apart: 1 -> 1, of which waited for: 0 -> 0; matrix products, arithmetic and copies ran while one was open for 2% -> 4% of each run, Pallas kernels for 0% -> 12%
where the time goes in v3:
time: 81.4 us; the launch traced here: 80.7 us
  Pallas kernels  51.2 us (63%)
  local copies, waits for them, and re-layouts  12.8 us (16%)
  other arithmetic  6.25 us (8%)
  matrix products  6.04 us (7%)
  starting transfers between devices  4.11 us (5%)
    pallas_call x1, Pallas kernels, carried_in(): pl.pallas_call(functools.partial(chain_kernel, devices), out_shape=jax.Sh...  35.9 us
    pallas_call x1, Pallas kernels, gate_sum(): pl.pallas_call(functools.partial(gate_kernel, groups), out_shape=jax.Shap...  9.61 us
    unnamed x35, local copies, waits for them, and re-layouts  8.12 us
    dot_general x7, matrix products, product(): return jnp.einsum(pattern, first_op, second_op, precision=highest)  6.04 us
    pallas_call x1, Pallas kernels, unit_lower_solve(): pl.pallas_call(solve_kernel, out_shape=jax.ShapeDtypeStruct(rhs.shape, jn...  5.59 us
    ppermute x1, starting transfers between devices, passed_along(): return lax.ppermute(value, axis, pairs)  4.11 us
  transfers between devices with their start and end apart: 1, of which 0 were waited for; matrix products, arithmetic and copies ran while one was open for 4% of the time, Pallas kernels for 12%

profile of v3, /device:TPU:7, one launch (start us, length us, event | category | flops | bytes accessed | tf_op | source)
XLA Modules:
  0.0 80.7 jit_solution(9467915802805226660)
XLA Ops:
  0.0 0.7 slice.133
  0.7 0.2 copy.121
  0.9 0.7 copy-done.5
  1.6 0.1 copy.119
  1.7 0.7 copy-done.6
  2.4 0.1 copy.120
  2.5 0.5 copy-done.11
  3.2 4.1 %collective-permute-start = (bf16[3,1025]{0,1:T(8,128)(2,1)S(1)}, bf16[3,1025]{0,1:T(8,128)(2,1)S(1)}, u32[]{:S(2)}, u32[]{:S(2)}) collective-permute-start(bf16[3,1025]{0,1:T(8,128)(2,1)S(1)} %pad_maximum_fusion), channel_id=1, source_target_pairs={{0,4},{4,8},{8,12},{12,16},{16,20},{20,24},{24,28},{28,32},{32,36}... | collective-permute-start | bytes 18458 | tf_op jit(solution)/shard_map/ppermute | solution.py:23
  7.4 0.6 copy-done.7
  8.0 0.8 copy.126.weight_ref
  8.8 9.6 %shard_map.127 = f32[128,16]{1,0:T(8,128)} custom-call(bf16[128,512]{1,0:T(8,128)(2,1)} %input_ref.1, bf16[512,16]{1,0:T(8,128)(2,1)} %copy.126.weight_ref), custom_call_target="tpu_custom_call" | custom-call | tf_op jit(solution)/shard_map/pallas_call | solution.py:283
  18.4 1.0 %fusion.34 = f32[128,2]{1,0:T(8,128)S(1)} fusion(f32[128,16]{1,0:T(8,128)} %shard_map.127, s32[]{:T(128)S(6)} %select_n.58, f32[2]{0:T(128)S(1)} %copy-done.12, f32[2]{0:T(128)S(1)} %neg.28), kind=kLoop, calls=%fused_computation.68 | loop fusion | flops 2048 | bytes 2068 | tf_op jit(solution)/shard_map/mul | solution.py:349
  19.4 0.2 reduce_window_sum.11
  19.6 0.5 copy-done.9
  20.1 0.7 copy-done.8
  20.8 0.7 copy-done.10
  21.5 0.6 slice.171
  22.2 0.1 copy.123
  22.3 0.7 copy-done.3
  22.9 0.1 copy.132
  23.1 0.7 copy-done.4
  23.8 0.1 copy.140
  24.1 0.5 copy-done.14
  24.7 0.6 slice.166
  25.3 1.3 %compare_convert_fusion = (f32[128]{0:T(128)S(1)}, f32[128]{0:T(128)S(1)}, pred[128]{0:T(512)(128)(4,1)S(1)}, pred[128]{0:T(512)(128)(4,1)S(1)}, pred[128]{0:T(512)(128)(4,1)S(1)}) fusion(s32[128]{0:T(128)S(1)} %copy-done.11, s32[]{:T(128)} %bitcast.24, s32[]{:T(128)} %bitcast.19, s32[131]{0:T(256)S(1)} %pad_add_fusion), kind=kLoop, calls=%fused_computation.86 | loop fusion | flops 896 | bytes 3464 | tf_op jit(solution)/shard_map/convert_element_type | solution.py:57
  26.7 0.6 slice.169
  27.3 0.1 fusion.44
  27.5 0.1 maximum_convert_fusion.1
  27.6 0.3 multiply_reduce_fusion.1
  28.2 0.1 maximum_convert_fusion
  28.3 0.6 divide_multiply_fusion
  28.9 0.1 copy.133
  29.2 0.7 exponential_multiply_fusion.2
  29.9 0.3 divide_multiply_fusion.2
  30.5 0.1 multiply_multiply_fusion
  30.6 0.8 maximum_bitcast_fusion.rhs_ref
  31.4 0.4 convolution_multiply_fusion.1
  31.8 1.1 %fusion.1.coupling_ref = f32[2,128,128]{2,1,0:T(8,128)} fusion(f32[128,2,128]{2,0,1:T(8,128)S(1)} %copy.124, f32[2,128]{1,0:T(2,128)S(1)} %copy.130, f32[2,128]{1,0:T(2,128)S(1)} %copy.128, f32[128,2]{0,1:T(2,128)S(1)} %add_rsqrt_fusion.1, pred[128,128]{1,0:T(8,128)(4,1)S(1)} %get-tuple-element.35, pred[128,128]{1,0:T(8,128)(4,1)S(1)} %get-tuple-element.36), kind=kOutput, calls=%fused_computation.5 | convolution fusion | flops 50561024 | bytes 297984 | tf_op jit(solution)/shard_map/ihd,jhd->hij/dot_general | solution.py:27
  33.0 5.6 %shard_map.128 = f32[2,128,384]{2,1,0:T(8,128)} custom-call(f32[2,128,128]{2,1,0:T(8,128)} %fusion.1.coupling_ref, f32[2,128,384]{2,1,0:T(8,128)} %maximum_bitcast_fusion.rhs_ref), custom_call_target="tpu_custom_call" | custom-call | tf_op jit(solution)/shard_map/pallas_call | solution.py:228
  38.6 2.2 %fusion.8.inject_ref = f32[2,128,256]{2,1,0:T(8,128)} fusion(f32[2,128,384]{2,1,0:T(8,128)} %shard_map.128, f32[128,2,128]{2,0,1:T(8,128)S(1)} %copy.124, f32[128,2]{0,1:T(2,128)S(1)} %copy.137, f32[128,2]{0,1:T(2,128)S(1)} %add_rsqrt_fusion.1), kind=kOutput, calls=%fused_computation.23 | convolution fusion | flops 100728832 | bytes 657408 | tf_op jit(solution)/shard_map/hcd,hce->hde/dot_general | solution.py:27
  40.8 0.4 fusion.10
  41.2 1.1 %convolution_subtract_fusion.carry_ref = f32[2,128,128]{2,1,0:T(8,128)} fusion(f32[2,128,384]{2,1,0:T(8,128)S(1)} %copy-done, f32[128,2,128]{2,0,1:T(8,128)S(1)} %copy.124, f32[128,2]{0,1:T(2,128)S(1)} %copy.137, f32[128,128]{1,0:T(8,128)S(1)} %fusion.41, f32[2]{0:T(128)S(1)} %exponential_multiply_fusion.2, f32[128,2]{0,1:T(2,128)S(1)} %add_rsqrt_fusion.1), kind=kOutput, calls=%fused_computation.2 | convolution fusion | flops 50462720 | bytes 461312 | tf_op jit(solution)/shard_map/hcd,hce->hde/dot_general | solution.py:27
  42.3 35.9 %shard_map.129 = f32[2,128,256]{2,1,0:T(8,128)} custom-call(f32[2,128,128]{2,1,0:T(8,128)} %convolution_subtract_fusion.carry_ref, f32[2,128,256]{2,1,0:T(8,128)} %fusion.8.inject_ref), custom_call_target="tpu_custom_call" | custom-call | tf_op jit(solution)/shard_map/pallas_call | solution.py:196
  78.3 0.3 convolution_subtract_fusion.1
  78.6 0.7 copy-done.1
  79.2 0.4 multiply_reduce_fusion
  79.8 0.1 copy.143
  79.9 0.8 copy.144
  (50 shorter events, 1.5 us)
Async XLA Ops:
  0.7 0.8 %copy-start.5 = (bf16[128,256]{1,0:T(8,128)(2,1)S(1)}, bf16[128,256]{1,0:T(8,128)(2,1)}, u32[]{:S(2)}) copy-start(bf16[128,256]{1,0:T(8,128)(2,1)} %param.14) | copy-start | bytes 196612
  1.5 0.8 %copy-start.6 = (bf16[128,256]{1,0:T(8,128)(2,1)S(1)}, bf16[128,256]{1,0:T(8,128)(2,1)}, u32[]{:S(2)}) copy-start(bf16[128,256]{1,0:T(8,128)(2,1)} %param.15) | copy-start | bytes 196612
  2.4 0.7 copy-start.11
  3.2 21.5 %collective-permute-start = (bf16[3,1025]{0,1:T(8,128)(2,1)S(1)}, bf16[3,1025]{0,1:T(8,128)(2,1)S(1)}, u32[]{:S(2)}, u32[]{:S(2)}) collective-permute-start(bf16[3,1025]{0,1:T(8,128)(2,1)S(1)} %pad_maximum_fusion), channel_id=1, source_target_pairs={{0,4},{4,8},{8,12},{12,16},{16,20},{20,24},{24,28},{28,32},{32,36}... | collective-permute-start | bytes 18458 | tf_op jit(solution)/shard_map/ppermute | solution.py:23
  7.3 0.7 copy-start.7
  8.0 0.8 copy-start.13
  8.8 9.6 %copy-start.12 = (f32[2]{0:T(128)S(1)}, f32[2]{0:T(128)}, u32[]{:S(2)}) copy-start(f32[2]{0:T(128)} %param.23) | copy-start | bytes 28
  19.4 0.7 copy-start.9
  20.1 0.7 copy-start.8
  20.8 0.7 copy-start.10
  22.0 0.9 %copy-start.3 = (bf16[128,512]{1,0:T(8,128)(2,1)S(1)}, bf16[128,512]{1,0:T(8,128)(2,1)}, u32[]{:S(2)}) copy-start(bf16[128,512]{1,0:T(8,128)(2,1)} %param.16) | copy-start | bytes 393220
  22.9 0.9 %copy-start.4 = (bf16[128,512]{1,0:T(8,128)(2,1)S(1)}, bf16[128,512]{1,0:T(8,128)(2,1)}, u32[]{:S(2)}) copy-start(bf16[128,512]{1,0:T(8,128)(2,1)} %param.17) | copy-start | bytes 393220
  24.0 0.7 copy-start.14
  24.0 3.3 %copy-start.2 = (f32[128,16]{1,0:T(8,128)S(1)}, f32[128,16]{1,0:T(8,128)}, u32[]{:S(2)}) copy-start(f32[128,16]{1,0:T(8,128)} %shard_map.127) | copy-start | bytes 24580
  38.5 2.2 %copy-start = (f32[2,128,384]{2,1,0:T(8,128)S(1)}, f32[2,128,384]{2,1,0:T(8,128)}, u32[]{:S(2)}) copy-start(f32[2,128,384]{2,1,0:T(8,128)} %shard_map.128) | copy-start | bytes 1179652
  78.3 1.0 %copy-start.1 = (f32[2,128,256]{2,1,0:T(8,128)S(1)}, f32[2,128,256]{2,1,0:T(8,128)}, u32[]{:S(2)}) copy-start(f32[2,128,256]{2,1,0:T(8,128)} %shard_map.129) | copy-start | bytes 786436

commit v4 on v3

--- a/solution.py
+++ b/solution.py
@@ -293,6 +293,103 @@
         ],
         compiler_params=pltpu.CompilerParams(collective_id=1, has_side_effects=True),
     )(layer_input, gate_weight)
+
+
+def fold_t(left, right):
+    return lax.dot_general(
+        left, right, (((1,), (1,)), ((), ())), precision=highest,
+        preferred_element_type=jnp.float32,
+    )
+
+
+def inverse_unit_lower(coupling, eye):
+    length = coupling.shape[0]
+    power = -coupling
+    inverse = eye + power
+    span = 2
+    while span < length:
+        power = fold(power, power)
+        inverse = inverse + fold(inverse, power)
+        span *= 2
+    return inverse
+
+
+def chunk_kernel(
+    ext_ref, seg_ref, taps_ref, gates_ref,
+    local_ref, reach_ref, carry_ref, inject_ref,
+):
+    length = local_ref.shape[1]
+    heads = local_ref.shape[0]
+    dk = carry_ref.shape[1]
+    dv = local_ref.shape[2]
+    edge = ext_ref.shape[0] - length
+    q_end = heads * dk
+    k_end = 2 * heads * dk
+
+    own_seg = seg_ref[pl.ds(edge, length), :]
+    summed = None
+    for offset in range(edge + 1):
+        term = jnp.where(
+            seg_ref[pl.ds(offset, length), :] == own_seg,
+            ext_ref[pl.ds(offset, length), :],
+            0.0,
+        ) * taps_ref[pl.ds(offset, 1), :]
+        summed = term if summed is None else summed + term
+    mixed_in = summed / (1.0 + jnp.exp(-summed))
+
+    rows = lax.broadcasted_iota(jnp.int32, (length, length), 0)
+    cols = lax.broadcasted_iota(jnp.int32, (length, length), 1)
+    eye = (rows == cols).astype(jnp.float32)
+    lower_ones = (rows >= cols).astype(jnp.float32)
+    seg_grid = jnp.broadcast_to(own_seg, (length, length))
+    same = seg_grid == jnp.transpose(seg_grid)
+    causal = (rows >= cols) & same
+    strict = (rows > cols) & same
+    linked = (own_seg == seg_ref[pl.ds(edge - 1, 1), :]).astype(jnp.float32)
+    tail = (own_seg == seg_ref[pl.ds(edge + length - 1, 1), :]).astype(jnp.float32)
+    linked_last = linked[length - 1 :, :]
+
+    for h in range(heads):
+        queries = mixed_in[:, h * dk : (h + 1) * dk]
+        key_raw = mixed_in[:, q_end + h * dk : q_end + (h + 1) * dk]
+        values = mixed_in[:, k_end + h * dv : k_end + (h + 1) * dv]
+        keys = key_raw * lax.rsqrt(jnp.sum(key_raw * key_raw, axis=1, keepdims=True) + 1e-06)
+        log_alpha = gates_ref[:, h : h + 1]
+        beta = gates_ref[:, heads + h : heads + h + 1]
+        cum_grid = fold(lower_ones, jnp.broadcast_to(log_alpha, (length, length)))
+        cumulative = cum_grid[:, 0:1]
+        last = cum_grid[length - 1 :, 0:1]
+        gap = cum_grid - jnp.transpose(cum_grid)
+        decays = jnp.where(causal, jnp.exp(jnp.where(causal, gap, 0.0)), 0.0)
+        coupling = beta * fold_t(keys, keys) * jnp.where(strict, decays, 0.0)
+        inverse = inverse_unit_lower(coupling, eye)
+        start_scale = jnp.exp(cumulative) * linked
+        fresh = fold(inverse, beta * values)
+        carried = fold(inverse, (beta * start_scale) * keys)
+        scores = fold_t(queries, keys) * decays
+        reach_ref[h] = queries * start_scale - fold(scores, carried)
+        local_ref[h] = fold(scores, fresh)
+        fade_out = jnp.exp(last - cumulative) * tail
+        pushed_t = jnp.transpose(fade_out * keys)
+        keep = linked_last * jnp.exp(last)
+        carry_ref[h] = keep * eye - fold(pushed_t, carried)
+        inject_ref[h] = fold(pushed_t, fresh)
+
+
+def chunk_terms(ext, seg_ext, taps, gates, heads):
+    length = ext.shape[0] - (CONV - 1)
+    shapes = (
+        jax.ShapeDtypeStruct((heads, length, DV), jnp.float32),
+        jax.ShapeDtypeStruct((heads, length, DK), jnp.float32),
+        jax.ShapeDtypeStruct((heads, DK, DK), jnp.float32),
+        jax.ShapeDtypeStruct((heads, DK, DV), jnp.float32),
+    )
+    return pl.pallas_call(
+        chunk_kernel,
+        out_shape=shapes,
+        in_specs=[pl.BlockSpec(memory_space=pltpu.VMEM)] * 4,
+        out_specs=[pl.BlockSpec(memory_space=pltpu.VMEM)] * 4,
+    )(ext, seg_ext, taps, gates)
 
 
 def local(
@@ -325,37 +422,21 @@
         axis=1,
     )
     prior = passed_along(edges, "req", 1)
-    prior_q = prior[:, :q_width]
-    prior_k = prior[:, q_width : q_width + k_width]
-    prior_v = prior[:, q_width + k_width : -1]
-    prior_seg = prior[:, -1].astype(jnp.int32) - 1
-    seg_ext = jnp.concatenate([prior_seg, segment_ids])
-    queries = short_conv(
-        jnp.concatenate([prior_q, q_in]).astype(jnp.float32), seg_ext, conv_q, row_count
-    )
-    keyset = unit_keys(
-        short_conv(
-            jnp.concatenate([prior_k, k_in]).astype(jnp.float32), seg_ext, conv_k, row_count
-        ),
-        local_heads,
-    )
-    values = short_conv(
-        jnp.concatenate([prior_v, v_in]).astype(jnp.float32), seg_ext, conv_v, row_count
-    )
+    prior_seg = prior[:, -1:].astype(jnp.float32) - 1.0
+    ext = jnp.concatenate(
+        [prior[:, :-1], jnp.concatenate([q_in, k_in, v_in], axis=1)], axis=0
+    ).astype(jnp.float32)
+    seg_ext = jnp.concatenate([prior_seg, segment_ids.astype(jnp.float32)[:, None]], axis=0)
+    taps = jnp.concatenate([conv_q, conv_k, conv_v], axis=1).astype(jnp.float32)
     gate_total = gate_sum(layer_input, gate_weight, lax.axis_size("tp"))
     head_start = lax.axis_index("tp") * local_heads
     decay_in = lax.dynamic_slice_in_dim(gate_total, head_start, local_heads, 1)
     beta_in = lax.dynamic_slice_in_dim(gate_total, HEADS + head_start, local_heads, 1)
     log_alpha = -decay_rate[None, :] * jax.nn.softplus(decay_in + dt_bias[None, :])
     beta_gate = jax.nn.sigmoid(beta_in)
-    local_out, reach_back, carry_map, injected = block_terms(
-        queries.reshape(row_count, local_heads, DK),
-        keyset,
-        values.reshape(row_count, local_heads, DV),
-        log_alpha,
-        beta_gate,
-        segment_ids,
-        prior_seg[edge_rows - 1],
+    gates = jnp.concatenate([log_alpha, beta_gate], axis=1)
+    local_out, reach_back, carry_map, injected = chunk_terms(
+        ext, seg_ext, taps, gates, local_heads
     )
     incoming = carried_in(carry_map, injected, lax.axis_size("req"))
     head_out = local_out + product("hcd,hde->hce", reach_back, incoming)

time: 81.4 us -> 68.9 us (0.85)
  local copies, waits for them, and re-layouts: 12.8 us -> 5.05 us
  matrix products: 6.04 us -> 1.41 us
  Pallas kernels: 51.2 us -> 53.6 us
  other arithmetic: 6.25 us -> 4.09 us
    unnamed x35 -> x30, local copies, waits for them, and re-layouts: 8.12 us -> 1.71 us
    dot_general x7 -> x1, matrix products: 6.04 us -> 1.41 us  [product(): return jnp.einsum(pattern, first_op, second_op, precision=highest)]
    pallas_call x1, Pallas kernels: 5.59 us -> 7.91 us  [chunk_terms(): pl.pallas_call(chunk_kernel, out_shape=shapes, in_specs=[pl.BlockSpec(mem...]
    mul x9 -> x0, other arithmetic: 1.94 us -> none  [the longest x2 0.89 us: short_conv(): return jax.nn.silu(summed)]
    slice x5 -> x1, local copies, waits for them, and re-layouts: 1.83 us -> 0.01 us  [local(): prior[:, :-1]]
    concatenate x1 -> x2, other arithmetic: 0.08 us -> 1.34 us  [the longest x1 0.71 us: local(): gates = jnp.concatenate([log_alpha, beta_gate], axis=1)]
    convert_element_type x4 -> x2, other arithmetic: 1.65 us -> 1.48 us  [the longest x1 0.87 us: local(): ext = jnp.concatenate([prior[:, :-1], jnp.concatenate([q_in, k_in, v_in],...]
  transfers between devices with their start and end apart: 1 -> 1, of which waited for: 0 -> 0; matrix products, arithmetic and copies ran while one was open for 4% -> 5% of each run, Pallas kernels for 12% -> 14%
where the time goes in v4:
time: 68.9 us; the launch traced here: 68.4 us
  Pallas kernels  53.6 us (78%)
  local copies, waits for them, and re-layouts  5.05 us (7%)
  starting transfers between devices  4.11 us (6%)
  other arithmetic  4.09 us (6%)
  matrix products  1.41 us (2%)
    pallas_call x1, Pallas kernels, carried_in(): pl.pallas_call(functools.partial(chain_kernel, devices), out_shape=jax.Sh...  36.4 us
    pallas_call x1, Pallas kernels, gate_sum(): pl.pallas_call(functools.partial(gate_kernel, groups), out_shape=jax.Shap...  9.3 us
    pallas_call x1, Pallas kernels, chunk_terms(): pl.pallas_call(chunk_kernel, out_shape=shapes, in_specs=[pl.BlockSpec(mem...  7.91 us
    ppermute x1, starting transfers between devices, passed_along(): return lax.ppermute(value, axis, pairs)  4.11 us
    unnamed x30, local copies, waits for them, and re-layouts  1.71 us
    dot_general x1, matrix products, product(): return jnp.einsum(pattern, first_op, second_op, precision=highest)  1.41 us
  transfers between devices with their start and end apart: 1, of which 0 were waited for; matrix products, arithmetic and copies ran while one was open for 5% of the time, Pallas kernels for 14%

profile of v4, /device:TPU:7, one launch (start us, length us, event | category | flops | bytes accessed | tf_op | source)
XLA Modules:
  0.0 68.4 jit_solution(13466729990683801830)
XLA Ops:
  0.0 0.7 %slice.20 = bf16[3,512]{1,0:T(4,128)(2,1)S(1)} slice(bf16[128,512]{1,0:T(8,128)(2,1)} %param.16), slice={[125:128], [0:512]} | slice | bytes 6144 | tf_op jit(solution)/shard_map/slice | solution.py:419
  0.7 0.7 %slice.18 = bf16[3,256]{1,0:T(4,128)(2,1)S(1)} slice(bf16[128,256]{1,0:T(8,128)(2,1)} %param.14), slice={[125:128], [0:256]} | slice | bytes 3072 | tf_op jit(solution)/shard_map/slice | solution.py:417
  1.4 0.0 copy-start.11
  1.4 0.7 %slice.19 = bf16[3,256]{1,0:T(4,128)(2,1)S(1)} slice(bf16[128,256]{1,0:T(8,128)(2,1)} %param.15), slice={[125:128], [0:256]} | slice | bytes 3072 | tf_op jit(solution)/shard_map/slice | solution.py:418
  2.1 0.0 copy-done.11
  2.1 0.1 convert_bitcast_fusion.1
  2.2 0.1 copy.46
  2.3 0.0 copy-start.6
  2.3 4.1 %collective-permute-start = (bf16[3,1025]{1,0:T(4,128)(2,1)S(1)}, bf16[3,1025]{1,0:T(4,128)(2,1)S(1)}, u32[]{:S(2)}, u32[]{:S(2)}) collective-permute-start(bf16[3,1025]{1,0:T(4,128)(2,1)S(1)} %pad_maximum_fusion.2), channel_id=1, source_target_pairs={{0,4},{4,8},{8,12},{12,16},{16,20},{20,24},{24,28},{28,32},{32,36}... | collective-permute-start | bytes 18458 | tf_op jit(solution)/shard_map/ppermute | solution.py:23
  6.4 0.0 copy-done.6
  6.4 0.0 copy-start.12
  6.5 0.8 %copy.48.weight_ref = bf16[512,16]{1,0:T(8,128)(2,1)} copy(bf16[512,16]{0,1:T(8,128)(2,1)S(1)} %copy-done.6) | data formatting | bytes 32768 | tf_op args[8]
  7.2 0.0 copy-done.12
  7.2 9.3 %shard_map.127 = f32[128,16]{1,0:T(8,128)} custom-call(bf16[128,512]{1,0:T(8,128)(2,1)} %input_ref.1, bf16[512,16]{1,0:T(8,128)(2,1)} %copy.48.weight_ref), custom_call_target="tpu_custom_call" | custom-call | tf_op jit(solution)/shard_map/pallas_call | solution.py:283
  16.5 0.0 copy-done.10
  16.5 1.1 %fusion.1 = (f32[128,2]{1,0:T(8,128)S(1)}, f32[128,2]{1,0:T(8,128)S(1)}) fusion(f32[128,16]{1,0:T(8,128)} %shard_map.127, s32[]{:T(128)S(6)} %select_n.10, f32[2]{0:T(128)S(1)} %copy-done.10, f32[2]{0:T(128)S(1)} %neg.15, s32[]{:T(128)S(6)} %select_n.12), kind=kLoop, calls=%fused_computation.7 | loop fusion | flops 2816 | bytes 4120 | tf_op jit(solution)/shard_map/mul | solution.py:435
  17.6 0.0 copy-start.7
  17.6 0.0 copy-start.8
  17.6 0.0 copy-start.9
  17.6 0.0 copy-start.2
  17.7 0.7 %pad_maximum_fusion.1.gates_ref = f32[128,4]{1,0:T(8,128)} fusion(f32[128,2]{1,0:T(8,128)S(1)} %get-tuple-element.14, f32[128,2]{1,0:T(8,128)S(1)} %get-tuple-element.13), kind=kLoop, calls=%fused_computation.8 | loop fusion | flops 512 | bytes 4096 | tf_op jit(solution)/shard_map/concatenate | solution.py:437
  18.4 0.0 copy-done.7
  18.4 0.0 copy-done.8
  18.4 0.0 copy-done.9
  18.4 0.6 maximum_convert_fusion.1.taps_ref
  19.0 0.1 copy.47
  19.1 0.0 copy-done.2
  19.1 0.1 copy.52
  19.2 0.0 copy-start.13
  19.2 0.0 copy-start.1
  19.2 0.0 copy-start.4
  19.2 0.0 copy-start.5
  19.3 0.1 copy.54
  19.4 0.5 copy-done.13
  19.9 0.0 collective-permute-done
  19.9 0.2 copy-done.1
  20.1 0.0 copy-done.4
  20.1 0.0 copy-done.5
  20.2 0.9 %maximum_convert_fusion.ext_ref = f32[131,1024]{1,0:T(8,128)} fusion(bf16[128,512]{1,0:T(8,128)(2,1)S(1)} %copy-done.1, bf16[128,256]{1,0:T(8,128)(2,1)S(1)} %copy-done.4, bf16[128,256]{1,0:T(8,128)(2,1)S(1)} %copy-done.5, bf16[3,1024]{1,0:T(4,128)(2,1)S(1)} %slice.24), kind=kLoop, calls=%fused_computation.2 | loop fusion | flops 1073152 | bytes 804864 | tf_op jit(solution)/shard_map/convert_element_type | solution.py:428
  21.0 0.6 pad_maximum_fusion.seg_ref
  21.7 7.9 %shard_map.128 = (f32[2,128,256]{2,1,0:T(8,128)}, f32[2,128,128]{2,1,0:T(8,128)}, f32[2,128,128]{2,1,0:T(8,128)}, f32[2,128,256]{2,1,0:T(8,128)}) custom-call(f32[131,1024]{1,0:T(8,128)} %maximum_convert_fusion.ext_ref, f32[131,1]{1,0:T(8,128)} %pad_maximum_fusion.seg_ref, f32[4,1024]{1,0:T(4,128)} %maximum_convert_fusion.1.taps_ref, ...), custom_call_target="tpu_custom_call" | custom-call | tf_op jit(solution)/shard_map/pallas_call | solution.py:387
  29.6 36.4 %shard_map.129 = f32[2,128,256]{2,1,0:T(8,128)} custom-call(f32[2,128,128]{2,1,0:T(8,128)} %get-tuple-element.11.carry_ref, f32[2,128,256]{2,1,0:T(8,128)} %get-tuple-element.12.inject_ref), custom_call_target="tpu_custom_call" | custom-call | tf_op jit(solution)/shard_map/pallas_call | solution.py:196
  66.0 0.0 copy-done
  66.0 0.0 copy-done.3
  66.0 1.4 %multiply_reduce_fusion = (f32[128,2]{0,1:T(2,128)S(1)}, f32[128,2,256]{2,0,1:T(8,128)S(1)}) fusion(f32[2,128,256]{2,1,0:T(8,128)S(1)} %copy-done, f32[2,128,128]{2,1,0:T(8,128)S(1)} %copy-done.3, f32[2,128,256]{2,1,0:T(8,128)} %shard_map.129), kind=kOutput, calls=%fused_computation.4 | convolution fusion | flops 100859648 | bytes 918528 | tf_op jit(solution)/shard_map/hcd,hde->hce/dot_general | solution.py:27
  67.4 0.1 multiply_convert_fusion
  67.5 0.1 copy.55
  67.7 0.8 %copy.56 = bf16[128,512]{1,0:T(8,128)(2,1)} copy(bf16[128,512]{0,1:T(8,128)(2,1)S(1)} %bitcast.12) | data formatting | bytes 262144 | tf_op jit(solution)/shard_map/reshape | solution.py:88
  (10 shorter events, 0.0 us)
Async XLA Ops:
  1.4 0.7 %copy-start.11 = (s32[128]{0:T(128)S(1)}, s32[128]{0:T(128)}, u32[]{:S(2)}) copy-start(s32[128]{0:T(128)} %param.25) | copy-start | bytes 1540
  2.3 4.2 %copy-start.6 = (bf16[512,16]{0,1:T(8,128)(2,1)S(1)}, bf16[512,16]{0,1:T(8,128)(2,1)}, u32[]{:S(2)}) copy-start(bf16[512,16]{0,1:T(8,128)(2,1)} %param.21) | copy-start | bytes 49156
  2.3 17.6 %collective-permute-start = (bf16[3,1025]{1,0:T(4,128)(2,1)S(1)}, bf16[3,1025]{1,0:T(4,128)(2,1)S(1)}, u32[]{:S(2)}, u32[]{:S(2)}) collective-permute-start(bf16[3,1025]{1,0:T(4,128)(2,1)S(1)} %pad_maximum_fusion.2), channel_id=1, source_target_pairs={{0,4},{4,8},{8,12},{12,16},{16,20},{20,24},{24,28},{28,32},{32,36}... | collective-permute-start | bytes 18458 | tf_op jit(solution)/shard_map/ppermute | solution.py:23
  6.4 0.8 %copy-start.12 = (f32[2]{0:T(128)S(1)}, f32[2]{0:T(128)}, u32[]{:S(2)}) copy-start(f32[2]{0:T(128)} %param.22) | copy-start | bytes 28
  7.2 9.3 %copy-start.10 = (f32[2]{0:T(128)S(1)}, f32[2]{0:T(128)}, u32[]{:S(2)}) copy-start(f32[2]{0:T(128)} %param.23) | copy-start | bytes 28
  17.6 0.8 %copy-start.7 = (bf16[4,512]{1,0:T(4,128)(2,1)S(1)}, bf16[4,512]{1,0:T(4,128)(2,1)}, u32[]{:S(2)}) copy-start(bf16[4,512]{1,0:T(4,128)(2,1)} %param.20) | copy-start | bytes 12292
  17.6 0.8 %copy-start.8 = (bf16[4,256]{1,0:T(4,128)(2,1)S(1)}, bf16[4,256]{1,0:T(4,128)(2,1)}, u32[]{:S(2)}) copy-start(bf16[4,256]{1,0:T(4,128)(2,1)} %param.19) | copy-start | bytes 6148
  17.6 0.7 %copy-start.9 = (bf16[4,256]{1,0:T(4,128)(2,1)S(1)}, bf16[4,256]{1,0:T(4,128)(2,1)}, u32[]{:S(2)}) copy-start(bf16[4,256]{1,0:T(4,128)(2,1)} %param.18) | copy-start | bytes 6148
  17.6 1.4 %copy-start.2 = (bf16[128,512]{1,0:T(8,128)(2,1)S(1)}, bf16[128,512]{1,0:T(8,128)(2,1)}, u32[]{:S(2)}) copy-start(bf16[128,512]{1,0:T(8,128)(2,1)} %param.17) | copy-start | bytes 393220
  19.2 0.7 copy-start.13
  19.2 0.9 %copy-start.1 = (bf16[128,512]{1,0:T(8,128)(2,1)S(1)}, bf16[128,512]{1,0:T(8,128)(2,1)}, u32[]{:S(2)}) copy-start(bf16[128,512]{1,0:T(8,128)(2,1)} %param.16) | copy-start | bytes 393220
  19.2 0.9 %copy-start.4 = (bf16[128,256]{1,0:T(8,128)(2,1)S(1)}, bf16[128,256]{1,0:T(8,128)(2,1)}, u32[]{:S(2)}) copy-start(bf16[128,256]{1,0:T(8,128)(2,1)} %param.15) | copy-start | bytes 196612
  19.2 0.9 %copy-start.5 = (bf16[128,256]{1,0:T(8,128)(2,1)S(1)}, bf16[128,256]{1,0:T(8,128)(2,1)}, u32[]{:S(2)}) copy-start(bf16[128,256]{1,0:T(8,128)(2,1)} %param.14) | copy-start | bytes 196612
  29.6 36.4 %copy-start = (f32[2,128,256]{2,1,0:T(8,128)S(1)}, f32[2,128,256]{2,1,0:T(8,128)}, u32[]{:S(2)}) copy-start(f32[2,128,256]{2,1,0:T(8,128)} %get-tuple-element.9) | copy-start | bytes 786436
  29.6 36.4 %copy-start.3 = (f32[2,128,128]{2,1,0:T(8,128)S(1)}, f32[2,128,128]{2,1,0:T(8,128)}, u32[]{:S(2)}) copy-start(f32[2,128,128]{2,1,0:T(8,128)} %get-tuple-element.10) | copy-start | bytes 393220

commit v5 on v4

--- a/solution.py
+++ b/solution.py
@@ -99,6 +99,7 @@
     devices, carry_ref, inject_ref, out_ref,
     got1_a, got1_b, got2_a, got2_b, got3_b, got4_b,
     lo_a, lo_b, join_a, join_b, pair_a, pair_b, quad_b, reply,
+    wire_a, wire_b, wire_pair, wire_quad,
     send_sems, recv_sems,
 ):
     me = lax.axis_index("req")
@@ -164,20 +165,24 @@
     hi_b = jnp.where(low, got1_b[...], own_b)
     join_a[...] = fold(hi_a, lo_a[...])
     join_b[...] = fold(hi_a, lo_b[...]) + hi_b
+    wire_a[...] = join_a[...].astype(wire_a.dtype)
+    wire_b[...] = join_b[...].astype(wire_b.dtype)
     for copy in first:
         copy.wait_send()
 
-    copies = along(1, ((join_a, got2_a), (join_b, got2_b)), 2)
-    pair_a[...] = fold(join_a[...], got2_a[...])
-    pair_b[...] = fold(join_a[...], got2_b[...]) + join_b[...]
+    copies = along(1, ((wire_a, got2_a), (wire_b, got2_b)), 2)
+    pair_a[...] = fold(join_a[...], got2_a[...].astype(jnp.float32))
+    pair_b[...] = fold(join_a[...], got2_b[...].astype(jnp.float32)) + join_b[...]
+    wire_pair[...] = pair_b[...].astype(wire_pair.dtype)
     sent(copies, 2)
 
-    copies = along(2, ((pair_b, got3_b),), 4)
-    quad_b[...] = fold(pair_a[...], got3_b[...]) + pair_b[...]
+    copies = along(2, ((wire_pair, got3_b),), 4)
+    quad_b[...] = fold(pair_a[...], got3_b[...].astype(jnp.float32)) + pair_b[...]
+    wire_quad[...] = quad_b[...].astype(wire_quad.dtype)
     sent(copies, 4)
 
-    copies = along(3, ((quad_b, got4_b),), 2)
-    entering = got4_b[...]
+    copies = along(3, ((wire_quad, got4_b),), 2)
+    entering = got4_b[...].astype(jnp.float32)
     onward = fold(lo_a[...], entering) + lo_b[...]
     sent(copies, 2)
 
@@ -193,14 +198,17 @@
     heads, dk, dv = inject_total.shape
     a_shape = pltpu.VMEM((dk, dk), jnp.float32)
     b_shape = pltpu.VMEM((dk, dv), jnp.float32)
+    a_wire = pltpu.VMEM((dk, dk), jnp.bfloat16)
+    b_wire = pltpu.VMEM((dk, dv), jnp.bfloat16)
     return pl.pallas_call(
         functools.partial(chain_kernel, devices),
         out_shape=jax.ShapeDtypeStruct((heads, dk, dv), jnp.float32),
         in_specs=[pl.BlockSpec(memory_space=pltpu.VMEM)] * 2,
         out_specs=pl.BlockSpec(memory_space=pltpu.VMEM),
         scratch_shapes=[
-            a_shape, b_shape, a_shape, b_shape, b_shape, b_shape,
+            a_shape, b_shape, a_wire, b_wire, b_wire, b_wire,
             a_shape, b_shape, a_shape, b_shape, a_shape, b_shape, b_shape, b_shape,
+            a_wire, b_wire, b_wire, b_wire,
             pltpu.SemaphoreType.DMA((5, 2)),
             pltpu.SemaphoreType.DMA((5, 2)),
         ],

time: 68.9 us -> 62.9 us (0.913)
  Pallas kernels: 53.6 us -> 47.5 us
    pallas_call x1, Pallas kernels: 36.4 us -> 30.3 us  [carried_in(): pl.pallas_call(functools.partial(chain_kernel, devices), out_shape=jax.Sh...]
  transfers between devices with their start and end apart: 1 -> 1, of which waited for: 0 -> 0; matrix products, arithmetic and copies ran while one was open for 5% -> 6% of each run, Pallas kernels for 14% -> 15%
where the time goes in v5:
time: 62.9 us; the launch traced here: 62.4 us
  Pallas kernels  47.5 us (76%)
  local copies, waits for them, and re-layouts  5.05 us (8%)
  starting transfers between devices  4.11 us (7%)
  other arithmetic  4.09 us (7%)
  matrix products  1.41 us (2%)
    pallas_call x1, Pallas kernels, carried_in(): pl.pallas_call(functools.partial(chain_kernel, devices), out_shape=jax.Sh...  30.3 us
    pallas_call x1, Pallas kernels, gate_sum(): pl.pallas_call(functools.partial(gate_kernel, groups), out_shape=jax.Shap...  9.3 us
    pallas_call x1, Pallas kernels, chunk_terms(): pl.pallas_call(chunk_kernel, out_shape=shapes, in_specs=[pl.BlockSpec(mem...  7.91 us
    ppermute x1, starting transfers between devices, passed_along(): return lax.ppermute(value, axis, pairs)  4.11 us
    unnamed x30, local copies, waits for them, and re-layouts  1.71 us
    dot_general x1, matrix products, product(): return jnp.einsum(pattern, first_op, second_op, precision=highest)  1.41 us
  transfers between devices with their start and end apart: 1, of which 0 were waited for; matrix products, arithmetic and copies ran while one was open for 6% of the time, Pallas kernels for 15%

profile of v5, /device:TPU:7, one launch (start us, length us, event | category | flops | bytes accessed | tf_op | source)
XLA Modules:
  0.0 62.4 jit_solution(15012388375880370443)
XLA Ops:
  0.0 0.7 %slice.20 = bf16[3,512]{1,0:T(4,128)(2,1)S(1)} slice(bf16[128,512]{1,0:T(8,128)(2,1)} %param.16), slice={[125:128], [0:512]} | slice | bytes 6144 | tf_op jit(solution)/shard_map/slice | solution.py:427
  0.7 0.7 %slice.18 = bf16[3,256]{1,0:T(4,128)(2,1)S(1)} slice(bf16[128,256]{1,0:T(8,128)(2,1)} %param.14), slice={[125:128], [0:256]} | slice | bytes 3072 | tf_op jit(solution)/shard_map/slice | solution.py:425
  1.4 0.0 copy-start.11
  1.4 0.7 %slice.19 = bf16[3,256]{1,0:T(4,128)(2,1)S(1)} slice(bf16[128,256]{1,0:T(8,128)(2,1)} %param.15), slice={[125:128], [0:256]} | slice | bytes 3072 | tf_op jit(solution)/shard_map/slice | solution.py:426
  2.1 0.0 copy-done.11
  2.1 0.1 convert_bitcast_fusion.1
  2.2 0.1 copy.46
  2.3 0.0 copy-start.6
  2.3 4.1 %collective-permute-start = (bf16[3,1025]{1,0:T(4,128)(2,1)S(1)}, bf16[3,1025]{1,0:T(4,128)(2,1)S(1)}, u32[]{:S(2)}, u32[]{:S(2)}) collective-permute-start(bf16[3,1025]{1,0:T(4,128)(2,1)S(1)} %pad_maximum_fusion.2), channel_id=1, source_target_pairs={{0,4},{4,8},{8,12},{12,16},{16,20},{20,24},{24,28},{28,32},{32,36}... | collective-permute-start | bytes 18458 | tf_op jit(solution)/shard_map/ppermute | solution.py:23
  6.4 0.0 copy-done.6
  6.4 0.0 copy-start.12
  6.5 0.8 %copy.48.weight_ref = bf16[512,16]{1,0:T(8,128)(2,1)} copy(bf16[512,16]{0,1:T(8,128)(2,1)S(1)} %copy-done.6) | data formatting | bytes 32768 | tf_op args[8]
  7.2 0.0 copy-done.12
  7.2 9.3 %shard_map.127 = f32[128,16]{1,0:T(8,128)} custom-call(bf16[128,512]{1,0:T(8,128)(2,1)} %input_ref.1, bf16[512,16]{1,0:T(8,128)(2,1)} %copy.48.weight_ref), custom_call_target="tpu_custom_call" | custom-call | tf_op jit(solution)/shard_map/pallas_call | solution.py:291
  16.5 0.0 copy-done.10
  16.5 1.1 %fusion.1 = (f32[128,2]{1,0:T(8,128)S(1)}, f32[128,2]{1,0:T(8,128)S(1)}) fusion(f32[128,16]{1,0:T(8,128)} %shard_map.127, s32[]{:T(128)S(6)} %select_n.10, f32[2]{0:T(128)S(1)} %copy-done.10, f32[2]{0:T(128)S(1)} %neg.15, s32[]{:T(128)S(6)} %select_n.12), kind=kLoop, calls=%fused_computation.7 | loop fusion | flops 2816 | bytes 4120 | tf_op jit(solution)/shard_map/mul | solution.py:443
  17.6 0.0 copy-start.7
  17.6 0.0 copy-start.8
  17.6 0.0 copy-start.9
  17.6 0.0 copy-start.2
  17.7 0.7 %pad_maximum_fusion.1.gates_ref = f32[128,4]{1,0:T(8,128)} fusion(f32[128,2]{1,0:T(8,128)S(1)} %get-tuple-element.14, f32[128,2]{1,0:T(8,128)S(1)} %get-tuple-element.13), kind=kLoop, calls=%fused_computation.8 | loop fusion | flops 512 | bytes 4096 | tf_op jit(solution)/shard_map/concatenate | solution.py:445
  18.4 0.0 copy-done.7
  18.4 0.0 copy-done.8
  18.4 0.0 copy-done.9
  18.4 0.6 maximum_convert_fusion.1.taps_ref
  19.0 0.1 copy.47
  19.1 0.0 copy-done.2
  19.1 0.1 copy.52
  19.2 0.0 copy-start.13
  19.2 0.0 copy-start.1
  19.2 0.0 copy-start.4
  19.2 0.0 copy-start.5
  19.3 0.1 copy.54
  19.4 0.5 copy-done.13
  19.9 0.0 collective-permute-done
  19.9 0.2 copy-done.1
  20.1 0.0 copy-done.4
  20.1 0.0 copy-done.5
  20.2 0.9 %maximum_convert_fusion.ext_ref = f32[131,1024]{1,0:T(8,128)} fusion(bf16[128,512]{1,0:T(8,128)(2,1)S(1)} %copy-done.1, bf16[128,256]{1,0:T(8,128)(2,1)S(1)} %copy-done.4, bf16[128,256]{1,0:T(8,128)(2,1)S(1)} %copy-done.5, bf16[3,1024]{1,0:T(4,128)(2,1)S(1)} %slice.24), kind=kLoop, calls=%fused_computation.2 | loop fusion | flops 1073152 | bytes 804864 | tf_op jit(solution)/shard_map/convert_element_type | solution.py:436
  21.0 0.6 %pad_maximum_fusion.seg_ref = f32[131,1]{1,0:T(8,128)} fusion(f32[128,1]{1,0:T(8,128)S(1)} %copy.47, f32[3,1]{1,0:T(4,128)S(1)} %convert_add_fusion), kind=kLoop, calls=%fused_computation.6 | loop fusion | flops 131 | bytes 1048 | tf_op jit(solution)/shard_map/concatenate | solution.py:437
  21.7 7.9 %shard_map.128 = (f32[2,128,256]{2,1,0:T(8,128)}, f32[2,128,128]{2,1,0:T(8,128)}, f32[2,128,128]{2,1,0:T(8,128)}, f32[2,128,256]{2,1,0:T(8,128)}) custom-call(f32[131,1024]{1,0:T(8,128)} %maximum_convert_fusion.ext_ref, f32[131,1]{1,0:T(8,128)} %pad_maximum_fusion.seg_ref, f32[4,1024]{1,0:T(4,128)} %maximum_convert_fusion.1.taps_ref, ...), custom_call_target="tpu_custom_call" | custom-call | tf_op jit(solution)/shard_map/pallas_call | solution.py:395
  29.6 30.3 %shard_map.129 = f32[2,128,256]{2,1,0:T(8,128)} custom-call(f32[2,128,128]{2,1,0:T(8,128)} %get-tuple-element.11.carry_ref, f32[2,128,256]{2,1,0:T(8,128)} %get-tuple-element.12.inject_ref), custom_call_target="tpu_custom_call" | custom-call | tf_op jit(solution)/shard_map/pallas_call | solution.py:203
  59.9 0.0 copy-done
  59.9 0.0 copy-done.3
  60.0 1.4 %multiply_reduce_fusion = (f32[128,2]{0,1:T(2,128)S(1)}, f32[128,2,256]{2,0,1:T(8,128)S(1)}) fusion(f32[2,128,256]{2,1,0:T(8,128)S(1)} %copy-done, f32[2,128,128]{2,1,0:T(8,128)S(1)} %copy-done.3, f32[2,128,256]{2,1,0:T(8,128)} %shard_map.129), kind=kOutput, calls=%fused_computation.4 | convolution fusion | flops 100859648 | bytes 918528 | tf_op jit(solution)/shard_map/hcd,hde->hce/dot_general | solution.py:27
  61.4 0.1 multiply_convert_fusion
  61.5 0.1 copy.55
  61.6 0.8 %copy.56 = bf16[128,512]{1,0:T(8,128)(2,1)} copy(bf16[128,512]{0,1:T(8,128)(2,1)S(1)} %bitcast.12) | data formatting | bytes 262144 | tf_op jit(solution)/shard_map/reshape | solution.py:88
  (10 shorter events, 0.0 us)
Async XLA Ops:
  1.4 0.7 %copy-start.11 = (s32[128]{0:T(128)S(1)}, s32[128]{0:T(128)}, u32[]{:S(2)}) copy-start(s32[128]{0:T(128)} %param.25) | copy-start | bytes 1540
  2.3 4.2 %copy-start.6 = (bf16[512,16]{0,1:T(8,128)(2,1)S(1)}, bf16[512,16]{0,1:T(8,128)(2,1)}, u32[]{:S(2)}) copy-start(bf16[512,16]{0,1:T(8,128)(2,1)} %param.21) | copy-start | bytes 49156
  2.3 17.6 %collective-permute-start = (bf16[3,1025]{1,0:T(4,128)(2,1)S(1)}, bf16[3,1025]{1,0:T(4,128)(2,1)S(1)}, u32[]{:S(2)}, u32[]{:S(2)}) collective-permute-start(bf16[3,1025]{1,0:T(4,128)(2,1)S(1)} %pad_maximum_fusion.2), channel_id=1, source_target_pairs={{0,4},{4,8},{8,12},{12,16},{16,20},{20,24},{24,28},{28,32},{32,36}... | collective-permute-start | bytes 18458 | tf_op jit(solution)/shard_map/ppermute | solution.py:23
  6.4 0.8 %copy-start.12 = (f32[2]{0:T(128)S(1)}, f32[2]{0:T(128)}, u32[]{:S(2)}) copy-start(f32[2]{0:T(128)} %param.22) | copy-start | bytes 28
  7.2 9.3 %copy-start.10 = (f32[2]{0:T(128)S(1)}, f32[2]{0:T(128)}, u32[]{:S(2)}) copy-start(f32[2]{0:T(128)} %param.23) | copy-start | bytes 28
  17.6 0.8 %copy-start.7 = (bf16[4,512]{1,0:T(4,128)(2,1)S(1)}, bf16[4,512]{1,0:T(4,128)(2,1)}, u32[]{:S(2)}) copy-start(bf16[4,512]{1,0:T(4,128)(2,1)} %param.20) | copy-start | bytes 12292
  17.6 0.8 %copy-start.8 = (bf16[4,256]{1,0:T(4,128)(2,1)S(1)}, bf16[4,256]{1,0:T(4,128)(2,1)}, u32[]{:S(2)}) copy-start(bf16[4,256]{1,0:T(4,128)(2,1)} %param.19) | copy-start | bytes 6148
  17.6 0.7 %copy-start.9 = (bf16[4,256]{1,0:T(4,128)(2,1)S(1)}, bf16[4,256]{1,0:T(4,128)(2,1)}, u32[]{:S(2)}) copy-start(bf16[4,256]{1,0:T(4,128)(2,1)} %param.18) | copy-start | bytes 6148
  17.6 1.4 %copy-start.2 = (bf16[128,512]{1,0:T(8,128)(2,1)S(1)}, bf16[128,512]{1,0:T(8,128)(2,1)}, u32[]{:S(2)}) copy-start(bf16[128,512]{1,0:T(8,128)(2,1)} %param.17) | copy-start | bytes 393220
  19.2 0.7 %copy-start.13 = (bf16[256]{0:T(256)(128)(2,1)S(1)}, bf16[256]{0:T(256)(128)(2,1)}, u32[]{:S(2)}) copy-start(bf16[256]{0:T(256)(128)(2,1)} %param.24) | copy-start | bytes 1540
  19.2 0.9 %copy-start.1 = (bf16[128,512]{1,0:T(8,128)(2,1)S(1)}, bf16[128,512]{1,0:T(8,128)(2,1)}, u32[]{:S(2)}) copy-start(bf16[128,512]{1,0:T(8,128)(2,1)} %param.16) | copy-start | bytes 393220
  19.2 0.9 %copy-start.4 = (bf16[128,256]{1,0:T(8,128)(2,1)S(1)}, bf16[128,256]{1,0:T(8,128)(2,1)}, u32[]{:S(2)}) copy-start(bf16[128,256]{1,0:T(8,128)(2,1)} %param.15) | copy-start | bytes 196612
  19.2 0.9 %copy-start.5 = (bf16[128,256]{1,0:T(8,128)(2,1)S(1)}, bf16[128,256]{1,0:T(8,128)(2,1)}, u32[]{:S(2)}) copy-start(bf16[128,256]{1,0:T(8,128)(2,1)} %param.14) | copy-start | bytes 196612
  29.6 30.4 %copy-start = (f32[2,128,256]{2,1,0:T(8,128)S(1)}, f32[2,128,256]{2,1,0:T(8,128)}, u32[]{:S(2)}) copy-start(f32[2,128,256]{2,1,0:T(8,128)} %get-tuple-element.9) | copy-start | bytes 786436
  29.6 30.4 %copy-start.3 = (f32[2,128,128]{2,1,0:T(8,128)S(1)}, f32[2,128,128]{2,1,0:T(8,128)}, u32[]{:S(2)}) copy-start(f32[2,128,128]{2,1,0:T(8,128)} %get-tuple-element.10) | copy-start | bytes 393220

commit v6 on v2

v6 whole, which is shorter than its diff:
```python
import functools

import jax
import jax.numpy as jnp
from jax import lax
from jax.experimental import pallas as pl
from jax.experimental.pallas import tpu as pltpu
from jax.sharding import PartitionSpec as P

HEADS = 8
DK = 128
DV = 256
CONV = 4
EDGE = 16

MESH = pl.DeviceIdType.MESH
highest = lax.Precision.HIGHEST


def fold(high, low):
    return jnp.dot(high, low, precision=highest, preferred_element_type=jnp.float32)


def fold_t(left, right):
    return lax.dot_general(
        left, right, (((1,), (1,)), ((), ())), precision=highest,
        preferred_element_type=jnp.float32,
    )


def inverse_unit_lower(coupling, eye):
    length = coupling.shape[0]
    power = -coupling
    inverse = eye + power
    span = 2
    while span < length:
        power = fold(power, power)
        inverse = inverse + fold(inverse, power)
        span *= 2
    return inverse


def layer_kernel(
    devices, groups,
    x_ref, w_ref, q_ref, k_ref, v_ref, z_ref, cq_ref, ck_ref, cv_ref,
    decay_ref, bias_ref, gain_ref, seg_ref,
    out_ref,
    partial, got_gate, prev_q, prev_k, prev_v, prev_seg,
    local_sc, reach_sc, carry_sc, inject_sc, incoming,
    got1_a, got1_b, got2_a, got2_b, got3_b, got4_b,
    lo_a, lo_b, join_a, join_b, pair_a, pair_b, quad_b, reply,
    wire_a, wire_b, wire_pair, wire_quad,
    gate_send, gate_recv, edge_send, edge_recv, send_sems, recv_sems,
):
    me = lax.axis_index("req")
    tp_me = lax.axis_index("tp")
    core = lax.rem(me, 2)
    partner = me + 1 - 2 * core
    length = q_ref.shape[0]
    heads = carry_sc.shape[0]

    def at(device):
        return (lax.rem(device + devices, devices), tp_me)

    def across(step):
        return (me, lax.rem(tp_me + step, groups))

    barrier = pltpu.get_barrier_semaphore()
    for shift in (1, 2, 4):
        for peer in (me + shift, me - shift):
            pl.semaphore_signal(barrier, inc=1, device_id=at(peer), device_id_type=MESH)
    for step in range(1, groups):
        pl.semaphore_signal(barrier, inc=1, device_id=across(step), device_id_type=MESH)
    pl.semaphore_wait(barrier, 6 + groups - 1)

    edge_pairs = (
        (q_ref.at[pl.ds(length - EDGE, EDGE), :], prev_q.at[pl.ds(length - EDGE, EDGE), :]),
        (k_ref.at[pl.ds(length - EDGE, EDGE), :], prev_k.at[pl.ds(length - EDGE, EDGE), :]),
        (v_ref.at[pl.ds(length - EDGE, EDGE), :], prev_v.at[pl.ds(length - EDGE, EDGE), :]),
        (seg_ref, prev_seg),
    )
    edge_copies = [
        pltpu.make_async_remote_copy(
            src_ref=src, dst_ref=dst, send_sem=edge_send.at[slot], recv_sem=edge_recv.at[slot],
            device_id=at(me + 1), device_id_type=MESH,
        )
        for slot, (src, dst) in enumerate(edge_pairs)
    ]

    @pl.when(me + 1 < devices)
    def _():
        for copy in edge_copies:
            copy.start()

    partial[...] = jnp.dot(x_ref[...], w_ref[...], preferred_element_type=jnp.float32)
    gate_copies = [
        pltpu.make_async_remote_copy(
            src_ref=partial, dst_ref=got_gate.at[tp_me], send_sem=gate_send.at[step],
            recv_sem=gate_recv.at[tp_me], device_id=across(step), device_id_type=MESH,
        )
        for step in range(1, groups)
    ]
    for copy in gate_copies:
        copy.start()

    for buffer in (prev_q, prev_k, prev_v):
        buffer[pl.ds(0, length - EDGE), :] = jnp.zeros(
            (length - EDGE, buffer.shape[1]), buffer.dtype
        )

    @pl.when(me >= 1)
    def _():
        for copy in edge_copies:
            copy.wait_recv()

    @pl.when(me < 1)
    def _():
        for buffer in (prev_q, prev_k, prev_v):
            buffer[pl.ds(length - EDGE, EDGE), :] = jnp.zeros(
                (EDGE, buffer.shape[1]), buffer.dtype
            )
        prev_seg[...] = jnp.full(prev_seg.shape, -1, prev_seg.dtype)

    rows = lax.broadcasted_iota(jnp.int32, (length, length), 0)
    cols = lax.broadcasted_iota(jnp.int32, (length, length), 1)
    eye = (rows == cols).astype(jnp.float32)
    lower_ones = (rows >= cols).astype(jnp.float32)
    seg_cols = jnp.transpose(jnp.broadcast_to(seg_ref[...].astype(jnp.float32), (length, length)))
    prev_cols = jnp.transpose(
        jnp.broadcast_to(prev_seg[...].astype(jnp.float32), (length, length))
    )
    own_seg = seg_cols[:, 0:1]
    token = rows[:, 0:1]

    def shifted(own, prev, shift):
        return jnp.where(token >= shift, pltpu.roll(own, shift, 0), pltpu.roll(prev, shift, 0))

    seg_before = [None] + [shifted(seg_cols, prev_cols, s)[:, 0:1] for s in range(1, CONV)]

    def short_conv(own_ref, prev_ref, taps_ref):
        own = own_ref[...].astype(jnp.float32)
        prev = prev_ref[...].astype(jnp.float32)
        summed = None
        for offset in range(CONV):
            shift = CONV - 1 - offset
            if shift == 0:
                term = own
            else:
                term = jnp.where(
                    seg_before[shift] == own_seg, shifted(own, prev, shift), 0.0
                )
            term = term * taps_ref[pl.ds(offset, 1), :].astype(jnp.float32)
            summed = term if summed is None else summed + term
        return summed / (1.0 + jnp.exp(-summed))

    queries_all = short_conv(q_ref, prev_q, cq_ref)
    keys_all = short_conv(k_ref, prev_k, ck_ref)
    values_all = short_conv(v_ref, prev_v, cv_ref)

    for step in range(1, groups):
        source = lax.rem(tp_me + step, groups)
        pltpu.make_async_remote_copy(
            src_ref=partial, dst_ref=got_gate.at[source], send_sem=gate_send.at[0],
            recv_sem=gate_recv.at[source], device_id=(me, source), device_id_type=MESH,
        ).wait_recv()
    gate_total = None
    for source in range(groups):
        term = jnp.where(source == tp_me, partial[...], got_gate[source])
        gate_total = term if gate_total is None else gate_total + term
    lanes = lax.broadcasted_iota(jnp.int32, gate_total.shape, 1)

    seg_grid = jnp.broadcast_to(own_seg, (length, length))
    same = seg_grid == jnp.transpose(seg_grid)
    causal = (rows >= cols) & same
    strict = (rows > cols) & same
    linked = (own_seg == prev_cols[length - 1 :, 0:1]).astype(jnp.float32)
    tail = (own_seg == own_seg[length - 1 :, :]).astype(jnp.float32)
    linked_last = linked[length - 1 :, :]

    for h in range(heads):
        column = tp_me * heads + h
        decay_in = jnp.sum(jnp.where(lanes == column, gate_total, 0.0), axis=1, keepdims=True)
        beta_in = jnp.sum(
            jnp.where(lanes == HEADS + column, gate_total, 0.0), axis=1, keepdims=True
        )
        shifted_in = decay_in + bias_ref[h]
        softplus = jnp.maximum(shifted_in, 0.0) + jnp.log1p(jnp.exp(-jnp.abs(shifted_in)))
        log_alpha = -decay_ref[h] * softplus
        beta = 1.0 / (1.0 + jnp.exp(-beta_in))

        queries = queries_all[:, h * DK : (h + 1) * DK]
        key_raw = keys_all[:, h * DK : (h + 1) * DK]
        values = values_all[:, h * DV : (h + 1) * DV]
        keys = key_raw * lax.rsqrt(jnp.sum(key_raw * key_raw, axis=1, keepdims=True) + 1e-06)
        cum_grid = fold(lower_ones, jnp.broadcast_to(log_alpha, (length, length)))
        cumulative = cum_grid[:, 0:1]
        last = cum_grid[length - 1 :, 0:1]
        gap = cum_grid - jnp.transpose(cum_grid)
        decays = jnp.where(causal, jnp.exp(jnp.where(causal, gap, 0.0)), 0.0)
        coupling = beta * fold_t(keys, keys) * jnp.where(strict, decays, 0.0)
        inverse = inverse_unit_lower(coupling, eye)
        start_scale = jnp.exp(cumulative) * linked
        fresh = fold(inverse, beta * values)
        carried = fold(inverse, (beta * start_scale) * keys)
        fade_out = jnp.exp(last - cumulative) * tail
        pushed_t = jnp.transpose(fade_out * keys)
        keep = linked_last * jnp.exp(last)
        carry_sc[h] = keep * eye - fold(pushed_t, carried)
        inject_sc[h] = fold(pushed_t, fresh)
        scores = fold_t(queries, keys) * decays
        reach_sc[h] = queries * start_scale - fold(scores, carried)
        local_sc[h] = fold(scores, fresh)

    for copy in gate_copies:
        copy.wait_send()

    @pl.when(me + 1 < devices)
    def _():
        for copy in edge_copies:
            copy.wait_send()

    def remote(step, slot, src, dst, target):
        return pltpu.make_async_remote_copy(
            src_ref=src, dst_ref=dst,
            send_sem=send_sems.at[step, slot], recv_sem=recv_sems.at[step, slot],
            device_id=at(target), device_id_type=MESH,
        )

    def along(step, pairs, shift):
        copies = [remote(step, slot, src, dst, me + shift) for slot, (src, dst) in enumerate(pairs)]

        @pl.when(me + shift < devices)
        def _():
            for copy in copies:
                copy.start()

        @pl.when(me >= shift)
        def _():
            for copy in copies:
                copy.wait_recv()

        @pl.when(me < shift)
        def _():
            for _, dst in pairs:
                dst[...] = jnp.zeros(dst.shape, dst.dtype)

        return copies

    def sent(copies, shift):
        @pl.when(me + shift < devices)
        def _():
            for copy in copies:
                copy.wait_send()

    first = [
        remote(0, 0, carry_sc.at[1 - core], got1_a, partner),
        remote(0, 1, inject_sc.at[1 - core], got1_b, partner),
    ]
    for copy in first:
        copy.start()
    for copy in first:
        copy.wait_recv()
    own_a = carry_sc[core]
    own_b = inject_sc[core]
    low = core == 0
    lo_a[...] = jnp.where(low, own_a, got1_a[...])
    lo_b[...] = jnp.where(low, own_b, got1_b[...])
    hi_a = jnp.where(low, got1_a[...], own_a)
    hi_b = jnp.where(low, got1_b[...], own_b)
    join_a[...] = fold(hi_a, lo_a[...])
    join_b[...] = fold(hi_a, lo_b[...]) + hi_b
    wire_a[...] = join_a[...].astype(wire_a.dtype)
    wire_b[...] = join_b[...].astype(wire_b.dtype)
    for copy in first:
        copy.wait_send()

    copies = along(1, ((wire_a, got2_a), (wire_b, got2_b)), 2)
    pair_a[...] = fold(join_a[...], got2_a[...].astype(jnp.float32))
    pair_b[...] = fold(join_a[...], got2_b[...].astype(jnp.float32)) + join_b[...]
    wire_pair[...] = pair_b[...].astype(wire_pair.dtype)
    sent(copies, 2)

    copies = along(2, ((wire_pair, got3_b),), 4)
    quad_b[...] = fold(pair_a[...], got3_b[...].astype(jnp.float32)) + pair_b[...]
    wire_quad[...] = quad_b[...].astype(wire_quad.dtype)
    sent(copies, 4)

    copies = along(3, ((wire_quad, got4_b),), 2)
    entering = got4_b[...].astype(jnp.float32)
    onward = fold(lo_a[...], entering) + lo_b[...]
    sent(copies, 2)

    reply[...] = jnp.where(low, onward, entering)
    last_copy = remote(4, 0, reply, incoming.at[core], partner)
    last_copy.start()
    incoming[core] = jnp.where(low, entering, onward)
    remote(4, 0, reply, incoming.at[1 - core], partner).wait_recv()

    gain = gain_ref[...].astype(jnp.float32)
    for h in range(heads):
        head_out = local_sc[h] + fold(reach_sc[h], incoming[h])
        scale = lax.rsqrt(jnp.mean(head_out * head_out, axis=1, keepdims=True) + 1e-06)
        z_part = z_ref[:, h * DV : (h + 1) * DV].astype(jnp.float32)
        gating = z_part / (1.0 + jnp.exp(-z_part))
        out_ref[:, h * DV : (h + 1) * DV] = (head_out * scale * gain * gating).astype(
            out_ref.dtype
        )
    last_copy.wait_send()


def local(
    layer_input, q_in, k_in, v_in, z_in, conv_q, conv_k, conv_v,
    gate_weight, decay_rate, dt_bias, norm_gain, segment_ids,
):
    length = q_in.shape[0]
    heads = q_in.shape[1] // DK
    devices = lax.axis_size("req")
    groups = lax.axis_size("tp")
    f32 = jnp.float32
    a_shape = pltpu.VMEM((DK, DK), f32)
    b_shape = pltpu.VMEM((DK, DV), f32)
    a_wire = pltpu.VMEM((DK, DK), jnp.bfloat16)
    b_wire = pltpu.VMEM((DK, DV), jnp.bfloat16)
    vmem = pl.BlockSpec(memory_space=pltpu.VMEM)
    smem = pl.BlockSpec(memory_space=pltpu.SMEM)
    return pl.pallas_call(
        functools.partial(layer_kernel, devices, groups),
        out_shape=jax.ShapeDtypeStruct(z_in.shape, jnp.bfloat16),
        in_specs=[vmem] * 9 + [smem, smem, vmem, vmem],
        out_specs=vmem,
        scratch_shapes=[
            pltpu.VMEM((length, gate_weight.shape[1]), f32),
            pltpu.VMEM((groups, length, gate_weight.shape[1]), f32),
            pltpu.VMEM(q_in.shape, q_in.dtype),
            pltpu.VMEM(k_in.shape, k_in.dtype),
            pltpu.VMEM(v_in.shape, v_in.dtype),
            pltpu.VMEM((1, length), segment_ids.dtype),
            pltpu.VMEM((heads, length, DV), f32),
            pltpu.VMEM((heads, length, DK), f32),
            pltpu.VMEM((heads, DK, DK), f32),
            pltpu.VMEM((heads, DK, DV), f32),
            pltpu.VMEM((heads, DK, DV), f32),
            a_shape, b_shape, a_wire, b_wire, b_wire, b_wire,
            a_shape, b_shape, a_shape, b_shape, a_shape, b_shape, b_shape, b_shape,
            a_wire, b_wire, b_wire, b_wire,
            pltpu.SemaphoreType.DMA((groups,)),
            pltpu.SemaphoreType.DMA((groups,)),
            pltpu.SemaphoreType.DMA((4,)),
            pltpu.SemaphoreType.DMA((4,)),
            pltpu.SemaphoreType.DMA((5, 2)),
            pltpu.SemaphoreType.DMA((5, 2)),
        ],
        compiler_params=pltpu.CompilerParams(collective_id=0, has_side_effects=True),
    )(
        layer_input, gate_weight, q_in, k_in, v_in, z_in, conv_q, conv_k, conv_v,
        decay_rate, dt_bias, norm_gain.reshape(1, -1), segment_ids.reshape(1, -1),
    )


def solution(mesh):
    placed = (
        P("req", "tp"),
        P("req", "tp"),
        P("req", "tp"),
        P("req", "tp"),
        P("req", "tp"),
        P(None, "tp"),
        P(None, "tp"),
        P(None, "tp"),
        P("tp", None),
        P("tp"),
        P("tp"),
        P(),
        P("req"),
    )
    return jax.shard_map(
        local, mesh=mesh, in_specs=placed, out_specs=P("req", "tp"), check_vma=False
    )
```

time: 79.9 us -> 48.6 us (0.61)
  blocking collectives: 9.26 us -> 0 us
  local copies, waits for them, and re-layouts: 12.7 us -> 4.28 us
  matrix products: 6.17 us -> 0 us
  other arithmetic: 5.33 us -> 0 us
  starting transfers between devices: 4.11 us -> 0 us
  Pallas kernels: 41.4 us -> 44.1 us
    psum x1 -> x0, blocking collectives: 9.26 us -> none  [local(): gate_total = lax.psum(partial_value, 'tp')]
    dot_general x8 -> x0, matrix products: 6.17 us -> none  [the longest x7 6.04 us: product(): return jnp.einsum(pattern, first_op, second_op, precision=highest)]
    unnamed x34 -> x4, local copies, waits for them, and re-layouts: 7.97 us -> 3.7 us
    ppermute x1 -> x0, starting transfers between devices: 4.11 us -> none  [passed_along(): return lax.ppermute(value, axis, pairs)]
    slice x11 -> x0, local copies, waits for them, and re-layouts: 3.07 us -> none  [the longest x2 0.91 us: local(): v_in[row_count - edge_rows:]]
    pallas_call x2 -> x1, Pallas kernels: 41.4 us -> 44.1 us  [local(): pl.pallas_call(functools.partial(layer_kernel, devices, groups), out_shap...]
    mul x11 -> x0, other arithmetic: 1.96 us -> none  [the longest x2 0.88 us: short_conv(): return jax.nn.silu(summed)]
    convert_element_type x6 -> x0, other arithmetic: 1.76 us -> none  [the longest x1 1.34 us: block_terms(): tail_mask = (seg_block == seg_block[length - 1]).astype(jnp.float32)]
  transfers between devices with their start and end apart: 1 -> 0, of which waited for: 0 -> 0; matrix products, arithmetic and copies ran while one was open for 2% -> 0% of each run, Pallas kernels for 0% -> 0%
where the time goes in v6:
time: 48.6 us; the launch traced here: 48.4 us
  Pallas kernels  44.1 us (91%)
  local copies, waits for them, and re-layouts  4.28 us (9%)
    pallas_call x1, Pallas kernels, local(): pl.pallas_call(functools.partial(layer_kernel, devices, groups), out_shap...  44.1 us
    unnamed x4, local copies, waits for them, and re-layouts  3.7 us

profile of v6, /device:TPU:7, one launch (start us, length us, event | category | flops | bytes accessed | tf_op | source)
XLA Modules:
  0.0 48.4 jit_solution(18321725531410648860)
XLA Ops:
  0.0 0.0 copy-start
  0.0 0.7 %copy-done = bf16[256]{0:T(256)(128)(2,1)S(1)} copy-done((bf16[256]{0:T(256)(128)(2,1)S(1)}, bf16[256]{0:T(256)(128)(2,1)}, u32[]{:S(2)}) %copy-start) | copy-done | bytes 536
  0.7 0.6 %reshape.6.gain_ref = bf16[1,256]{1,0:T(2,128)(2,1)} reshape(bf16[256]{0:T(256)(128)(2,1)S(1)} %copy-done) | data formatting | bytes 1024 | tf_op jit(solution)/shard_map/reshape | solution.py:356
  1.2 1.5 %copy.14.w_ref = bf16[512,16]{1,0:T(8,128)(2,1)} copy(bf16[512,16]{0,1:T(8,128)(2,1)} %param.21) | data formatting | bytes 32768 | tf_op args[8]
  2.7 44.1 %shard_map.127 = bf16[128,512]{1,0:T(8,128)(2,1)} custom-call(bf16[128,512]{1,0:T(8,128)(2,1)} %x_ref.1, bf16[512,16]{1,0:T(8,128)(2,1)} %copy.14.w_ref, bf16[128,256]{1,0:T(8,128)(2,1)} %q_ref.1, bf16[128,256]{1,0:T(8,128)(2,1)} %k_ref.1, bf16[128,512]{1,0:T(8,128)(2,1)} %v_ref.1, bf16[128,512]{1,0:T(8,128)(2,1)} %z_ref.1, bf16[4,256]{1,0:T(4,128)(2,1)} %cq_ref.1, ...), custom_call_target="tpu_custom_call" | custom-call | tf_op jit(solution)/shard_map/pallas_call | solution.py:326
  46.8 1.6 %copy.16 = bf16[128,512]{1,0:T(8,128)(2,1)} copy(bf16[128,512]{1,0:T(8,128)(2,1)} %shard_map.127) | data formatting | bytes 262144
Async XLA Ops:
  0.0 0.7 %copy-start = (bf16[256]{0:T(256)(128)(2,1)S(1)}, bf16[256]{0:T(256)(128)(2,1)}, u32[]{:S(2)}) copy-start(bf16[256]{0:T(256)(128)(2,1)} %param.24) | copy-start | bytes 1540

commit v7 on v6

--- a/solution.py
+++ b/solution.py
@@ -47,6 +47,7 @@
     out_ref,
     partial, got_gate, prev_q, prev_k, prev_v, prev_seg,
     local_sc, reach_sc, carry_sc, inject_sc, incoming,
+    keys_sc, decay_sc, start_sc, fresh_sc, carried_sc,
     got1_a, got1_b, got2_a, got2_b, got3_b, got4_b,
     lo_a, lo_b, join_a, join_b, pair_a, pair_b, quad_b, reply,
     wire_a, wire_b, wire_pair, wire_quad,
@@ -177,7 +178,7 @@
     tail = (own_seg == own_seg[length - 1 :, :]).astype(jnp.float32)
     linked_last = linked[length - 1 :, :]
 
-    for h in range(heads):
+    def head_terms(h):
         column = tp_me * heads + h
         decay_in = jnp.sum(jnp.where(lanes == column, gate_total, 0.0), axis=1, keepdims=True)
         beta_in = jnp.sum(
@@ -188,7 +189,6 @@
         log_alpha = -decay_ref[h] * softplus
         beta = 1.0 / (1.0 + jnp.exp(-beta_in))
 
-        queries = queries_all[:, h * DK : (h + 1) * DK]
         key_raw = keys_all[:, h * DK : (h + 1) * DK]
         values = values_all[:, h * DV : (h + 1) * DV]
         keys = key_raw * lax.rsqrt(jnp.sum(key_raw * key_raw, axis=1, keepdims=True) + 1e-06)
@@ -207,17 +207,17 @@
         keep = linked_last * jnp.exp(last)
         carry_sc[h] = keep * eye - fold(pushed_t, carried)
         inject_sc[h] = fold(pushed_t, fresh)
-        scores = fold_t(queries, keys) * decays
-        reach_sc[h] = queries * start_scale - fold(scores, carried)
-        local_sc[h] = fold(scores, fresh)
-
-    for copy in gate_copies:
-        copy.wait_send()
-
-    @pl.when(me + 1 < devices)
-    def _():
-        for copy in edge_copies:
-            copy.wait_send()
+        keys_sc[h] = keys
+        decay_sc[h] = decays
+        start_sc[h] = jnp.broadcast_to(start_scale, (length, DK))
+        fresh_sc[h] = fresh
+        carried_sc[h] = carried
+
+    def head_outputs(h):
+        queries = queries_all[:, h * DK : (h + 1) * DK]
+        scores = fold_t(queries, keys_sc[h]) * decay_sc[h]
+        reach_sc[h] = queries * start_sc[h] - fold(scores, carried_sc[h])
+        local_sc[h] = fold(scores, fresh_sc[h])
 
     def remote(step, slot, src, dst, target):
         return pltpu.make_async_remote_copy(
@@ -226,7 +226,7 @@
             device_id=at(target), device_id_type=MESH,
         )
 
-    def along(step, pairs, shift):
+    def launch(step, pairs, shift):
         copies = [remote(step, slot, src, dst, me + shift) for slot, (src, dst) in enumerate(pairs)]
 
         @pl.when(me + shift < devices)
@@ -234,6 +234,9 @@
             for copy in copies:
                 copy.start()
 
+        return copies
+
+    def land(copies, pairs, shift):
         @pl.when(me >= shift)
         def _():
             for copy in copies:
@@ -256,8 +259,23 @@
         remote(0, 0, carry_sc.at[1 - core], got1_a, partner),
         remote(0, 1, inject_sc.at[1 - core], got1_b, partner),
     ]
-    for copy in first:
-        copy.start()
+    for own_head in range(heads):
+
+        @pl.when(core == own_head)
+        def _():
+            head_terms(1 - own_head)
+            for copy in first:
+                copy.start()
+            head_terms(own_head)
+
+    for copy in gate_copies:
+        copy.wait_send()
+
+    @pl.when(me + 1 < devices)
+    def _():
+        for copy in edge_copies:
+            copy.wait_send()
+
     for copy in first:
         copy.wait_recv()
     own_a = carry_sc[core]
@@ -274,18 +292,26 @@
     for copy in first:
         copy.wait_send()
 
-    copies = along(1, ((wire_a, got2_a), (wire_b, got2_b)), 2)
+    pairs = ((wire_a, got2_a), (wire_b, got2_b))
+    copies = launch(1, pairs, 2)
+    head_outputs(0)
+    land(copies, pairs, 2)
     pair_a[...] = fold(join_a[...], got2_a[...].astype(jnp.float32))
     pair_b[...] = fold(join_a[...], got2_b[...].astype(jnp.float32)) + join_b[...]
     wire_pair[...] = pair_b[...].astype(wire_pair.dtype)
     sent(copies, 2)
 
-    copies = along(2, ((wire_pair, got3_b),), 4)
+    pairs = ((wire_pair, got3_b),)
+    copies = launch(2, pairs, 4)
+    head_outputs(1)
+    land(copies, pairs, 4)
     quad_b[...] = fold(pair_a[...], got3_b[...].astype(jnp.float32)) + pair_b[...]
     wire_quad[...] = quad_b[...].astype(wire_quad.dtype)
     sent(copies, 4)
 
-    copies = along(3, ((wire_quad, got4_b),), 2)
+    pairs = ((wire_quad, got4_b),)
+    copies = launch(3, pairs, 2)
+    land(copies, pairs, 2)
     entering = got4_b[...].astype(jnp.float32)
     onward = fold(lo_a[...], entering) + lo_b[...]
     sent(copies, 2)
@@ -340,6 +366,11 @@
             pltpu.VMEM((heads, DK, DK), f32),
             pltpu.VMEM((heads, DK, DV), f32),
             pltpu.VMEM((heads, DK, DV), f32),
+            pltpu.VMEM((heads, length, DK), f32),
+            pltpu.VMEM((heads, length, length), f32),
+            pltpu.VMEM((heads, length, DK), f32),
+            pltpu.VMEM((heads, length, DV), f32),
+            pltpu.VMEM((heads, length, DK), f32),
             a_shape, b_shape, a_wire, b_wire, b_wire, b_wire,
             a_shape, b_shape, a_shape, b_shape, a_shape, b_shape, b_shape, b_shape,
             a_wire, b_wire, b_wire, b_wire,

time: 48.6 us -> 45.8 us (0.942)
  Pallas kernels: 44.1 us -> 41.3 us
    pallas_call x1, Pallas kernels: 44.1 us -> 41.3 us  [local(): pl.pallas_call(functools.partial(layer_kernel, devices, groups), out_shap...]
where the time goes in v7:
time: 45.8 us; the launch traced here: 45.6 us
  Pallas kernels  41.3 us (90%)
  local copies, waits for them, and re-layouts  4.28 us (9%)
    pallas_call x1, Pallas kernels, local(): pl.pallas_call(functools.partial(layer_kernel, devices, groups), out_shap...  41.3 us
    unnamed x4, local copies, waits for them, and re-layouts  3.7 us

profile of v7, /device:TPU:7, one launch (start us, length us, event | category | flops | bytes accessed | tf_op | source)
XLA Modules:
  0.0 45.6 jit_solution(12206838817103044183)
XLA Ops:
  0.0 0.0 copy-start
  0.0 0.7 %copy-done = bf16[256]{0:T(256)(128)(2,1)S(1)} copy-done((bf16[256]{0:T(256)(128)(2,1)S(1)}, bf16[256]{0:T(256)(128)(2,1)}, u32[]{:S(2)}) %copy-start) | copy-done | bytes 536
  0.7 0.6 %reshape.6.gain_ref = bf16[1,256]{1,0:T(2,128)(2,1)} reshape(bf16[256]{0:T(256)(128)(2,1)S(1)} %copy-done) | data formatting | bytes 1024 | tf_op jit(solution)/shard_map/reshape | solution.py:387
  1.2 1.5 %copy.14.w_ref = bf16[512,16]{1,0:T(8,128)(2,1)} copy(bf16[512,16]{0,1:T(8,128)(2,1)} %param.21) | data formatting | bytes 32768 | tf_op args[8]
  2.7 41.3 %shard_map.127 = bf16[128,512]{1,0:T(8,128)(2,1)} custom-call(bf16[128,512]{1,0:T(8,128)(2,1)} %x_ref.1, bf16[512,16]{1,0:T(8,128)(2,1)} %copy.14.w_ref, bf16[128,256]{1,0:T(8,128)(2,1)} %q_ref.1, bf16[128,256]{1,0:T(8,128)(2,1)} %k_ref.1, bf16[128,512]{1,0:T(8,128)(2,1)} %v_ref.1, bf16[128,512]{1,0:T(8,128)(2,1)} %z_ref.1, bf16[4,256]{1,0:T(4,128)(2,1)} %cq_ref.1, ...), custom_call_target="tpu_custom_call" | custom-call | tf_op jit(solution)/shard_map/pallas_call | solution.py:352
  44.1 1.6 %copy.16 = bf16[128,512]{1,0:T(8,128)(2,1)} copy(bf16[128,512]{1,0:T(8,128)(2,1)} %shard_map.127) | data formatting | bytes 262144
Async XLA Ops:
  0.0 0.7 %copy-start = (bf16[256]{0:T(256)(128)(2,1)S(1)}, bf16[256]{0:T(256)(128)(2,1)}, u32[]{:S(2)}) copy-start(bf16[256]{0:T(256)(128)(2,1)} %param.24) | copy-start | bytes 1540

commit v8 on v7

--- a/solution.py
+++ b/solution.py
@@ -67,12 +67,22 @@
         return (me, lax.rem(tp_me + step, groups))
 
     barrier = pltpu.get_barrier_semaphore()
+    expected = groups - 1
     for shift in (1, 2, 4):
-        for peer in (me + shift, me - shift):
-            pl.semaphore_signal(barrier, inc=1, device_id=at(peer), device_id_type=MESH)
+
+        @pl.when(me + shift < devices)
+        def _():
+            pl.semaphore_signal(barrier, inc=1, device_id=at(me + shift), device_id_type=MESH)
+
+        @pl.when(me >= shift)
+        def _():
+            pl.semaphore_signal(barrier, inc=1, device_id=at(me - shift), device_id_type=MESH)
+
+        expected = expected + (me + shift < devices).astype(jnp.int32)
+        expected = expected + (me >= shift).astype(jnp.int32)
     for step in range(1, groups):
         pl.semaphore_signal(barrier, inc=1, device_id=across(step), device_id_type=MESH)
-    pl.semaphore_wait(barrier, 6 + groups - 1)
+    pl.semaphore_wait(barrier, expected)
 
     edge_pairs = (
         (q_ref.at[pl.ds(length - EDGE, EDGE), :], prev_q.at[pl.ds(length - EDGE, EDGE), :]),

time: 45.8 us -> 45.9 us (level)
  no operation moved by 1% of the time
where the time goes in v8:
time: 45.9 us; the launch traced here: 45.7 us
  Pallas kernels  41.4 us (90%)
  local copies, waits for them, and re-layouts  4.28 us (9%)
    pallas_call x1, Pallas kernels, local(): pl.pallas_call(functools.partial(layer_kernel, devices, groups), out_shap...  41.4 us
    unnamed x4, local copies, waits for them, and re-layouts  3.7 us

profile of v8, /device:TPU:7, one launch (start us, length us, event | category | flops | bytes accessed | tf_op | source)
XLA Modules:
  0.0 45.7 jit_solution(7520646586193404641)
XLA Ops:
  0.0 0.0 copy-start
  0.0 0.7 %copy-done = bf16[256]{0:T(256)(128)(2,1)S(1)} copy-done((bf16[256]{0:T(256)(128)(2,1)S(1)}, bf16[256]{0:T(256)(128)(2,1)}, u32[]{:S(2)}) %copy-start) | copy-done | bytes 536
  0.7 0.6 %reshape.6.gain_ref = bf16[1,256]{1,0:T(2,128)(2,1)} reshape(bf16[256]{0:T(256)(128)(2,1)S(1)} %copy-done) | data formatting | bytes 1024 | tf_op jit(solution)/shard_map/reshape | solution.py:397
  1.2 1.5 %copy.14.w_ref = bf16[512,16]{1,0:T(8,128)(2,1)} copy(bf16[512,16]{0,1:T(8,128)(2,1)} %param.21) | data formatting | bytes 32768 | tf_op args[8]
  2.7 41.4 %shard_map.127 = bf16[128,512]{1,0:T(8,128)(2,1)} custom-call(bf16[128,512]{1,0:T(8,128)(2,1)} %x_ref.1, bf16[512,16]{1,0:T(8,128)(2,1)} %copy.14.w_ref, bf16[128,256]{1,0:T(8,128)(2,1)} %q_ref.1, bf16[128,256]{1,0:T(8,128)(2,1)} %k_ref.1, bf16[128,512]{1,0:T(8,128)(2,1)} %v_ref.1, bf16[128,512]{1,0:T(8,128)(2,1)} %z_ref.1, bf16[4,256]{1,0:T(4,128)(2,1)} %cq_ref.1, ...), custom_call_target="tpu_custom_call" | custom-call | tf_op jit(solution)/shard_map/pallas_call | solution.py:362
  44.1 1.6 %copy.16 = bf16[128,512]{1,0:T(8,128)(2,1)} copy(bf16[128,512]{1,0:T(8,128)(2,1)} %shard_map.127) | data formatting | bytes 262144
Async XLA Ops:
  0.0 0.7 %copy-start = (bf16[256]{0:T(256)(128)(2,1)S(1)}, bf16[256]{0:T(256)(128)(2,1)}, u32[]{:S(2)}) copy-start(bf16[256]{0:T(256)(128)(2,1)} %param.24) | copy-start | bytes 1540
